TPU v7x, 32 devices: a whole 2x2x4 slice. The times are simulated.
32 devices in a mesh: ctx: 8 (over y, x, core), head: 4 (over z).
Axes of the slice: x: 2, y: 2, z: 4, core: 2. Of those that a mesh axis runs over, the one named last changes fastest.
Arguments:
- queries: bfloat16 [4096, 4096], P(('ctx', 'head')), may hold values from -34 to 34
- key_rows: bfloat16 [4096, 2048], P(('ctx', 'head')), may hold values from -34 to 34
- value_rows: bfloat16 [4096, 2048], P(('ctx', 'head')), may hold values from -6 to 6
- out_grad: bfloat16 [4096, 4096], P(('ctx', 'head')), may hold values from -6 to 6
Outputs:
- query_grad: bfloat16 [4096, 4096], P(('ctx', 'head'))
- key_grad: bfloat16 [4096, 2048], P(('ctx', 'head'))
- value_grad: bfloat16 [4096, 2048], P(('ctx', 'head'))
All inputs are finite; a program needn't handle non-finite values.
Results may differ from a plain program's by a relative error of at most 0.0072.
Values may be sent and summed in bfloat16 or wider, within the bound.
No kernel may reach another device: no remote copies, remote signals or barrier semaphores. Data moves between devices by JAX's collectives and lax.ppermute only.
A program may use at most 128 MiB of HBM per device.

v0:
```python
import functools

import jax
import jax.numpy as jnp
from jax import lax
from jax.experimental import pallas as pl
from jax.experimental.pallas import tpu as pltpu
from jax.sharding import PartitionSpec as P


HEAD_DIM = 128
Q_HEADS = 32
KV_HEADS = 16
WINDOW = 1024
GROUPS = Q_HEADS // KV_HEADS
Q_COLS = GROUPS * HEAD_DIM
TILE = 128

score_scale = 168.0 ** (-0.5)
LOG2_E = 1.4426950408889634


def vmem():
    return pl.BlockSpec(memory_space=pltpu.VMEM)


def smem():
    return pl.BlockSpec(memory_space=pltpu.SMEM)


def moved_bytes(arrays):
    return sum(a.size * a.dtype.itemsize for a in arrays)


def local_call(body, outs, args, flops=0, transcendentals=0, scratch=()):
    return pl.pallas_call(
        body,
        out_shape=outs,
        in_specs=[smem()] + [vmem()] * (len(args) - 1),
        out_specs=[vmem()] * len(outs),
        scratch_shapes=list(scratch),
        cost_estimate=pl.CostEstimate(
            flops=flops,
            transcendentals=transcendentals,
            bytes_accessed=moved_bytes(list(args[1:]) + list(outs)),
        ),
    )(*args)


def across(shard, parts, step):
    return lax.ppermute(shard, "head", [(i, i ^ step) for i in range(parts)])


def shifted(shard, by):
    count = lax.axis_size("ctx")
    pairs = [(i, i + by) for i in range(count) if 0 <= i + by < count]
    return lax.ppermute(shard, "ctx", pairs)


def pack_two(parts, width, chunks, place, left, right, *outs):
    for step in range(parts):
        partner = jnp.bitwise_xor(place[0], step)
        for chunk in range(chunks):
            out = outs[step * chunks + chunk]
            start = pl.multiple_of((partner * chunks + chunk) * width, width)
            out[:, 0:width] = left[:, pl.ds(start, width)]
            out[:, width : 2 * width] = right[:, pl.ds(start, width)]


def join_rows(parts, chunks, place, *refs):
    outs = refs[parts:]
    rows = refs[0].shape[0]
    for step in range(parts):
        partner = jnp.bitwise_xor(place[0], step)
        at = pl.ds(pl.multiple_of(partner * rows, rows), rows)
        for chunk in range(chunks):
            for side in range(2):
                start = (side * chunks + chunk) * HEAD_DIM
                outs[chunk][at, side * HEAD_DIM : (side + 1) * HEAD_DIM] = refs[step][
                    :, start : start + HEAD_DIM
                ]


def attend(parts, place, far, near, own, *refs):
    pieces = refs[:parts]
    dq_out, own_out, near_out, far_out = refs[parts : parts + 4]
    q_rows, g_rows, keys, values, keys_t, score, d_att, att_low, d_low, dk, dv = refs[parts + 4 :]
    rows = pieces[0].shape[0]
    block = rows * parts
    span = score.shape[0]
    tiles = span // TILE
    for step in range(parts):
        partner = jnp.bitwise_xor(place[0], step)
        at = pl.ds(pl.multiple_of(partner * rows, rows), rows)
        q_rows[at, :] = pieces[step][:, 0:Q_COLS]
        g_rows[at, :] = pieces[step][:, Q_COLS : 2 * Q_COLS]
    for i, kv in enumerate((far, near, own)):
        there = slice(i * block, (i + 1) * block)
        keys[there, :] = kv[:, 0:HEAD_DIM]
        values[there, :] = kv[:, HEAD_DIM : 2 * HEAD_DIM]
        keys_t[:, there] = kv[:, 0:HEAD_DIM].T
    dk[...] = jnp.zeros_like(dk)
    dv[...] = jnp.zeros_like(dv)
    first_key = WINDOW - place[1] * block
    lanes = GROUPS * TILE
    key_id = lax.broadcasted_iota(jnp.int32, (TILE, lanes), 0)
    row_id = jnp.bitwise_and(lax.broadcasted_iota(jnp.int32, (TILE, lanes), 1), TILE - 1)
    lower = key_id <= row_id
    across_cols = (((1,), (1,)), ((), ()))
    exponent = jnp.float32(score_scale * LOG2_E)

    def fold(x):
        return x.reshape(TILE // 8, 8, lanes)

    for row_block in range(block // TILE):
        base = row_block * TILE
        these = slice(base, base + TILE)
        q_two = jnp.concatenate(
            [q_rows[these, g * HEAD_DIM : (g + 1) * HEAD_DIM] for g in range(GROUPS)], axis=0
        )
        g_two = jnp.concatenate(
            [g_rows[these, g * HEAD_DIM : (g + 1) * HEAD_DIM] for g in range(GROUPS)], axis=0
        )
        top = jnp.full((8, lanes), -1e30, jnp.float32)
        for t in range(tiles):
            s = lax.dot_general(
                keys[base + t * TILE : base + (t + 1) * TILE, :],
                q_two,
                across_cols,
                preferred_element_type=jnp.float32,
            )
            if t == 0:
                s = jnp.where(lower, -1e30, s)
            if t == tiles - 1:
                s = jnp.where(lower, s, -1e30)
            score[t * TILE : (t + 1) * TILE, :] = s
            gone = jnp.where(base + t * TILE < first_key, -1e30, 0.0)
            top = jnp.maximum(top, jnp.max(fold(s), axis=0) + gone)
        top = jnp.max(top, axis=0, keepdims=True)
        total = jnp.zeros((8, lanes), jnp.float32)
        inner = jnp.zeros((8, lanes), jnp.float32)
        for t in range(tiles):
            here = slice(t * TILE, (t + 1) * TILE)
            level = top + jnp.where(base + t * TILE < first_key, 1e30, 0.0)
            p = jnp.exp2((score[here, :] - level) * exponent)
            score[here, :] = p
            total = total + jnp.sum(fold(p), axis=0)
            d = lax.dot_general(
                values[base + t * TILE : base + (t + 1) * TILE, :],
                g_two,
                across_cols,
                preferred_element_type=jnp.float32,
            )
            d_att[here, :] = d
            inner = inner + jnp.sum(fold(p * d), axis=0)
        inverse = 1.0 / jnp.sum(total, axis=0, keepdims=True)
        center = jnp.sum(inner, axis=0, keepdims=True) * inverse
        for t in range(tiles):
            here = slice(t * TILE, (t + 1) * TILE)
            att = score[here, :] * inverse
            att_low[here, :] = att.astype(jnp.bfloat16)
            d_low[here, :] = (att * (d_att[here, :] - center)).astype(jnp.bfloat16)
        there = slice(base, base + span)
        dv[there, :] += jnp.dot(att_low[...], g_two, preferred_element_type=jnp.float32)
        dk[there, :] += jnp.dot(d_low[...], q_two, preferred_element_type=jnp.float32)
        dq_t = jnp.dot(keys_t[:, there], d_low[...], preferred_element_type=jnp.float32)
        dq = (dq_t * score_scale).T.astype(jnp.bfloat16)
        for g in range(GROUPS):
            dq_out[these, g * HEAD_DIM : (g + 1) * HEAD_DIM] = dq[g * TILE : (g + 1) * TILE, :]
    for out, start in ((far_out, 0), (near_out, block), (own_out, 2 * block)):
        out[:, 0:HEAD_DIM] = (dk[start : start + block, :] * score_scale).astype(out.dtype)
        out[:, HEAD_DIM : 2 * HEAD_DIM] = dv[start : start + block, :].astype(out.dtype)


def add_up(parts, place, dq, own, near, far, *outs):
    rows = outs[0].shape[0]
    for step in range(parts):
        partner = jnp.bitwise_xor(place[0], step)
        at = pl.ds(pl.multiple_of(partner * rows, rows), rows)
        outs[step][:, 0:Q_COLS] = dq[at, :]
        total = own[at, :] + near[at, :].astype(jnp.float32) + far[at, :].astype(jnp.float32)
        outs[step][:, Q_COLS : Q_COLS + 2 * HEAD_DIM] = total.astype(jnp.bfloat16)


def unpack(parts, chunks, place, *refs):
    pieces = refs[: parts * chunks]
    dq, dk, dv = refs[parts * chunks :]
    for step in range(parts):
        partner = jnp.bitwise_xor(place[0], step)
        for chunk in range(chunks):
            piece = pieces[step * chunks + chunk]
            slot = partner * chunks + chunk
            dq[:, pl.ds(pl.multiple_of(slot * Q_COLS, Q_COLS), Q_COLS)] = piece[:, 0:Q_COLS]
            at = pl.ds(pl.multiple_of(slot * HEAD_DIM, HEAD_DIM), HEAD_DIM)
            dk[:, at] = piece[:, Q_COLS : Q_COLS + HEAD_DIM]
            dv[:, at] = piece[:, Q_COLS + HEAD_DIM : Q_COLS + 2 * HEAD_DIM]


def shards(queries, key_rows, value_rows, out_grad):
    parts = lax.axis_size("head")
    rows = queries.shape[0]
    block = rows * parts
    chunks = KV_HEADS // parts
    key_count = WINDOW + block
    span = WINDOW + TILE
    low, wide = jnp.bfloat16, jnp.float32
    place = jnp.stack([lax.axis_index("head"), lax.axis_index("ctx")]).astype(jnp.int32)
    kv_width = chunks * HEAD_DIM

    kv_piece = jax.ShapeDtypeStruct((rows, 2 * kv_width), low)
    kv_pieces = local_call(
        functools.partial(pack_two, parts, kv_width, 1),
        [kv_piece] * parts,
        (place, key_rows, value_rows),
    )
    kv_pieces = [kv_pieces[0]] + [across(kv_pieces[s], parts, s) for s in range(1, parts)]
    q_piece = jax.ShapeDtypeStruct((rows, 2 * Q_COLS), low)
    q_pieces = local_call(
        functools.partial(pack_two, parts, Q_COLS, chunks),
        [q_piece] * (parts * chunks),
        (place, queries, out_grad),
    )
    arrived = {}
    for chunk in range(chunks):
        for step in range(parts):
            piece = q_pieces[step * chunks + chunk]
            if step:
                piece = across(piece, parts, step)
            arrived[chunk, step] = piece

    half = jax.ShapeDtypeStruct((block, 2 * HEAD_DIM), low)
    kv_own = local_call(
        functools.partial(join_rows, parts, chunks), [half] * chunks, (place, *kv_pieces)
    )
    kv_near = [shifted(kv_own[c], 1) for c in range(chunks)]
    kv_far = [shifted(kv_own[c], 2) for c in range(chunks)]

    full = jax.ShapeDtypeStruct((block, 2 * HEAD_DIM), wide)
    lanes = GROUPS * TILE
    pairs = block * span * GROUPS
    back = {}
    for chunk in range(chunks):
        pieces = [arrived[chunk, step] for step in range(parts)]
        sources = [kv_far[chunk], kv_near[chunk], kv_own[chunk]]
        outs = [half, full, half, half]
        call = functools.partial(
            local_call,
            functools.partial(attend, parts),
            outs,
            flops=10 * pairs * HEAD_DIM,
            transcendentals=pairs,
            scratch=[
                pltpu.VMEM((block, Q_COLS), low),
                pltpu.VMEM((block, Q_COLS), low),
                pltpu.VMEM((key_count, HEAD_DIM), low),
                pltpu.VMEM((key_count, HEAD_DIM), low),
                pltpu.VMEM((HEAD_DIM, key_count), low),
                pltpu.VMEM((span, lanes), wide),
                pltpu.VMEM((span, lanes), wide),
                pltpu.VMEM((span, lanes), low),
                pltpu.VMEM((span, lanes), low),
                pltpu.VMEM((key_count, HEAD_DIM), wide),
                pltpu.VMEM((key_count, HEAD_DIM), wide),
            ],
        )
        dq, own, near, far = call((place, *sources, *pieces))
        near = shifted(near, -1)
        far = shifted(far, -2)
        sent = local_call(
            functools.partial(add_up, parts), [q_piece] * parts, (place, dq, own, near, far)
        )
        for step in range(parts):
            piece = sent[step]
            if step:
                piece = across(piece, parts, step)
            back[step * chunks + chunk] = piece
    return tuple(
        local_call(
            functools.partial(unpack, parts, chunks),
            [
                jax.ShapeDtypeStruct(queries.shape, low),
                jax.ShapeDtypeStruct(key_rows.shape, low),
                jax.ShapeDtypeStruct(value_rows.shape, low),
            ],
            (place, *[back[i] for i in range(parts * chunks)]),
        )
    )


def solution(mesh):
    spec = P(("ctx", "head"), None)
    return jax.shard_map(
        shards,
        mesh=mesh,
        in_specs=(spec, spec, spec, spec),
        out_specs=(spec, spec, spec),
        check_vma=False,
    )
```

profile of v0, /device:TPU:6, one launch (start us, length us, event | category | flops | bytes accessed | tf_op | source)
XLA Modules:
  0.0 192.8 jit_solution(10961275446360112587)
XLA Ops:
  1.3 3.1 %shard_map.69 = (bf16[128,512]{1,0:T(8,128)(2,1)}, bf16[128,512]{1,0:T(8,128)(2,1)}, bf16[128,512]{1,0:T(8,128)(2,1)}, bf16[128,512]{1,0:T(8,128)(2,1)}, bf16[12...) custom-call(s32[2]{0:T(128)} %pad_add_fusion.place, ...), custom_call_target="tpu_custom_call" | custom-call | bytes 4194304 | tf_op jit(solution)/shard_map/pallas_call | solution.py:36
  6.1 2.3 %shard_map.67 = (bf16[128,1024]{1,0:T(8,128)(2,1)}, bf16[128,1024]{1,0:T(8,128)(2,1)}, bf16[128,1024]{1,0:T(8,128)(2,1)}, bf16[128,1024]{1,0:T(8,128)(2,1)}) custom-call(s32[2]{0:T(128)} %pad_add_fusion.place, bf16[128,2048]{1,0:T(8,128)(2,1)} %left.2, bf16[128,2048]{1,0:T(8,128)(2,1)} %right.2), custom_call_target="tpu_custom_call" | custom-call | bytes 2097152 | tf_op jit(solution)/shard_map/pallas_call | solution.py:36
  8.8 2.6 %collective-permute-start.1 = (bf16[128,1024]{1,0:T(8,128)(2,1)}, bf16[128,1024]{1,0:T(8,128)(2,1)S(1)}, u32[]{:S(2)}, u32[]{:S(2)}) collective-permute-start(bf16[128,1024]{1,0:T(8,128)(2,1)} %get-tuple-element.61), channel_id=1, source_target_pairs={{0,2},{1,3},{2,0},{3,1},{4,6},{5,7},{6,4},{7,5},{8,10},{9,11},{10,... | collective-permute-start | bytes 786440 | tf_op jit(solution)/shard_map/ppermute | solution.py:51
  15.4 28.9 %collective-permute-done.27.refs_2_ = bf16[128,512]{1,0:T(8,128)(2,1)S(1)} collective-permute-done((bf16[128,512]{1,0:T(8,128)(2,1)S(1)}, bf16[128,512]{1,0:T(8,128)(2,1)S(1)}, u32[]{:S(2)}, u32[]{:S(2)}) %collective-permute-start.27) | collective-permute-done | bytes 131104 | tf_op jit(solution)/shard_map/ppermute | solution.py:51
  44.9 4.4 %collective-permute-start.20 = (bf16[128,512]{1,0:T(8,128)(2,1)S(1)}, bf16[128,512]{1,0:T(8,128)(2,1)S(1)}, u32[]{:S(2)}, u32[]{:S(2)}) collective-permute-start(bf16[128,512]{1,0:T(8,128)(2,1)S(1)} %copy-done.53), channel_id=1, source_target_pairs={{0,2},{1,3},{2,0},{3,1},{4,6},{5,7},{6,4},{7,5},{8,10},{9,11},{10,... | collective-permute-start | bytes 393224 | tf_op jit(solution)/shard_map/ppermute | solution.py:51
  50.0 3.9 %collective-permute-start.13 = (bf16[128,512]{1,0:T(8,128)(2,1)S(1)}, bf16[128,512]{1,0:T(8,128)(2,1)S(1)}, u32[]{:S(2)}, u32[]{:S(2)}) collective-permute-start(bf16[128,512]{1,0:T(8,128)(2,1)S(1)} %copy-done.48), channel_id=1, source_target_pairs={{0,2},{1,3},{2,0},{3,1},{4,6},{5,7},{6,4},{7,5},{8,10},{9,11},{10,... | collective-permute-start | bytes 393224 | tf_op jit(solution)/shard_map/ppermute | solution.py:51
  53.9 2.4 %shard_map.68 = (bf16[512,256]{1,0:T(8,128)(2,1)}, bf16[512,256]{1,0:T(8,128)(2,1)}, bf16[512,256]{1,0:T(8,128)(2,1)}, bf16[512,256]{1,0:T(8,128)(2,1)}) custom-call(s32[2]{0:T(128)} %pad_add_fusion.place, bf16[128,1024]{1,0:T(8,128)(2,1)} %get-tuple-element.59.refs_0_, bf16[128,1024]{1,0:T(8,128)(2,1)} %copy-done.8, bf16[128,1024]{1,0:T(8,128)(2,1)} %copy-done.9, ...), custom_call_target="tpu_custom_call" | custom-call | bytes 2097152 | tf_op jit(solution)/shard_map/pallas_call | solution.py:36
  61.1 3.6 %collective-permute-start.14 = (bf16[128,512]{1,0:T(8,128)(2,1)S(1)}, bf16[128,512]{1,0:T(8,128)(2,1)S(1)}, u32[]{:S(2)}, u32[]{:S(2)}) collective-permute-start(bf16[128,512]{1,0:T(8,128)(2,1)S(1)} %copy-done.47), channel_id=1, source_target_pairs={{0,3},{1,2},{2,1},{3,0},{4,7},{5,6},{6,5},{7,4},{8,11},{9,10},{10,... | collective-permute-start | bytes 393224 | tf_op jit(solution)/shard_map/ppermute | solution.py:51
  66.8 3.6 %collective-permute-done.13.refs_2_ = bf16[128,512]{1,0:T(8,128)(2,1)S(1)} collective-permute-done((bf16[128,512]{1,0:T(8,128)(2,1)S(1)}, bf16[128,512]{1,0:T(8,128)(2,1)S(1)}, u32[]{:S(2)}, u32[]{:S(2)}) %collective-permute-start.13) | collective-permute-done | bytes 131104 | tf_op jit(solution)/shard_map/ppermute | solution.py:51
  74.1 5.7 %collective-permute-done.6.refs_2_ = bf16[128,512]{1,0:T(8,128)(2,1)S(1)} collective-permute-done((bf16[128,512]{1,0:T(8,128)(2,1)S(1)}, bf16[128,512]{1,0:T(8,128)(2,1)S(1)}, u32[]{:S(2)}, u32[]{:S(2)}) %collective-permute-start.6) | collective-permute-done | bytes 131104 | tf_op jit(solution)/shard_map/ppermute | solution.py:51
  84.3 6.9 %shard_map.76 = (bf16[512,256]{1,0:T(8,128)(2,1)}, f32[512,256]{1,0:T(8,128)}, bf16[512,256]{1,0:T(8,128)(2,1)}, bf16[512,256]{1,0:T(8,128)(2,1)}) custom-call(s32[2]{0:T(128)} %pad_add_fusion.place, bf16[512,256]{1,0:T(8,128)(2,1)} %copy-done.27, bf16[512,256]{1,0:T(8,128)(2,1)} %copy-done.31, bf16[512,256]{1,0:T(8,128)(2,1)} %get-tuple-element.93.own, ...), custom_call_target="tpu_custom_call" | custom-call | flops 1509949440 | bytes 2621440 | tf_op jit(solution)/shard_map/pallas_call | solution.py:36
  95.2 4.5 %collective-permute-start.29 = (bf16[512,256]{1,0:T(8,128)(2,1)}, bf16[512,256]{1,0:T(8,128)(2,1)S(1)}, u32[]{:S(2)}, u32[]{:S(2)}) collective-permute-start(bf16[512,256]{1,0:T(8,128)(2,1)} %get-tuple-element.100), channel_id=1, source_target_pairs={{4,0},{8,4},{12,8},{16,12},{20,16},{24,20},{28,24},{5,1},{9,5},{13... | collective-permute-start | bytes 786440 | tf_op jit(solution)/shard_map/ppermute | solution.py:57
  99.7 6.9 %shard_map.74 = (bf16[512,256]{1,0:T(8,128)(2,1)}, f32[512,256]{1,0:T(8,128)}, bf16[512,256]{1,0:T(8,128)(2,1)}, bf16[512,256]{1,0:T(8,128)(2,1)}) custom-call(s32[2]{0:T(128)} %pad_add_fusion.place, bf16[512,256]{1,0:T(8,128)(2,1)} %copy-done.30, bf16[512,256]{1,0:T(8,128)(2,1)} %copy-done.33, bf16[512,256]{1,0:T(8,128)(2,1)} %get-tuple-element.83.own, ...), custom_call_target="tpu_custom_call" | custom-call | flops 1509949440 | bytes 2621440 | tf_op jit(solution)/shard_map/pallas_call | solution.py:36
  106.6 5.5 %collective-permute-start.30 = (bf16[512,256]{1,0:T(8,128)(2,1)S(1)}, bf16[512,256]{1,0:T(8,128)(2,1)S(1)}, u32[]{:S(2)}, u32[]{:S(2)}) collective-permute-start(bf16[512,256]{1,0:T(8,128)(2,1)S(1)} %copy-done.24), channel_id=1, source_target_pairs={{8,0},{12,4},{16,8},{20,12},{24,16},{28,20},{9,1},{13,5},{17,9},{2... | collective-permute-start | bytes 786440 | tf_op jit(solution)/shard_map/ppermute | solution.py:57
  114.2 6.9 %shard_map.72 = (bf16[512,256]{1,0:T(8,128)(2,1)}, f32[512,256]{1,0:T(8,128)}, bf16[512,256]{1,0:T(8,128)(2,1)}, bf16[512,256]{1,0:T(8,128)(2,1)}) custom-call(s32[2]{0:T(128)} %pad_add_fusion.place, bf16[512,256]{1,0:T(8,128)(2,1)} %copy-done.29, bf16[512,256]{1,0:T(8,128)(2,1)} %copy-done.32, bf16[512,256]{1,0:T(8,128)(2,1)} %get-tuple-element.73.own, ...), custom_call_target="tpu_custom_call" | custom-call | flops 1509949440 | bytes 2621440 | tf_op jit(solution)/shard_map/pallas_call | solution.py:36
  121.1 3.7 %collective-permute-start.23 = (bf16[512,256]{1,0:T(8,128)(2,1)S(1)}, bf16[512,256]{1,0:T(8,128)(2,1)S(1)}, u32[]{:S(2)}, u32[]{:S(2)}) collective-permute-start(bf16[512,256]{1,0:T(8,128)(2,1)S(1)} %copy-done.25), channel_id=1, source_target_pairs={{8,0},{12,4},{16,8},{20,12},{24,16},{28,20},{9,1},{13,5},{17,9},{2... | collective-permute-start | bytes 786440 | tf_op jit(solution)/shard_map/ppermute | solution.py:57
  129.1 6.8 %shard_map.70 = (bf16[512,256]{1,0:T(8,128)(2,1)}, f32[512,256]{1,0:T(8,128)}, bf16[512,256]{1,0:T(8,128)(2,1)}, bf16[512,256]{1,0:T(8,128)(2,1)}) custom-call(s32[2]{0:T(128)} %pad_add_fusion.place, bf16[512,256]{1,0:T(8,128)(2,1)} %copy-done.26, bf16[512,256]{1,0:T(8,128)(2,1)} %copy-done.28, bf16[512,256]{1,0:T(8,128)(2,1)} %get-tuple-element.63.own, ...), custom_call_target="tpu_custom_call" | custom-call | flops 1509949440 | bytes 2621440 | tf_op jit(solution)/shard_map/pallas_call | solution.py:36
  142.1 3.2 %collective-permute-start.38 = (bf16[128,512]{1,0:T(8,128)(2,1)}, bf16[128,512]{1,0:T(8,128)(2,1)S(1)}, u32[]{:S(2)}, u32[]{:S(2)}) collective-permute-start(bf16[128,512]{1,0:T(8,128)(2,1)} %get-tuple-element.110), channel_id=1, source_target_pairs={{0,2},{1,3},{2,0},{3,1},{4,6},{5,7},{6,4},{7,5},{8,10},{9,11},{10,... | collective-permute-start | bytes 393224 | tf_op jit(solution)/shard_map/ppermute | solution.py:51
  151.1 3.2 %collective-permute-start.37 = (bf16[128,512]{1,0:T(8,128)(2,1)S(1)}, bf16[128,512]{1,0:T(8,128)(2,1)S(1)}, u32[]{:S(2)}, u32[]{:S(2)}) collective-permute-start(bf16[128,512]{1,0:T(8,128)(2,1)S(1)} %copy-done.59), channel_id=1, source_target_pairs={{0,2},{1,3},{2,0},{3,1},{4,6},{5,7},{6,4},{7,5},{8,10},{9,11},{10,... | collective-permute-start | bytes 393224 | tf_op jit(solution)/shard_map/ppermute | solution.py:51
  157.9 7.6 %collective-permute-start.36 = (bf16[128,512]{1,0:T(8,128)(2,1)S(1)}, bf16[128,512]{1,0:T(8,128)(2,1)S(1)}, u32[]{:S(2)}, u32[]{:S(2)}) collective-permute-start(bf16[128,512]{1,0:T(8,128)(2,1)S(1)} %copy-done.58), channel_id=1, source_target_pairs={{0,2},{1,3},{2,0},{3,1},{4,6},{5,7},{6,4},{7,5},{8,10},{9,11},{10,... | collective-permute-start | bytes 393224 | tf_op jit(solution)/shard_map/ppermute | solution.py:51
  166.2 4.4 %collective-permute-done.37.refs_10_ = bf16[128,512]{1,0:T(8,128)(2,1)S(1)} collective-permute-done((bf16[128,512]{1,0:T(8,128)(2,1)S(1)}, bf16[128,512]{1,0:T(8,128)(2,1)S(1)}, u32[]{:S(2)}, u32[]{:S(2)}) %collective-permute-start.37) | collective-permute-done | bytes 131104 | tf_op jit(solution)/shard_map/ppermute | solution.py:51
  170.6 6.1 %collective-permute-start.35 = (bf16[128,512]{1,0:T(8,128)(2,1)}, bf16[128,512]{1,0:T(8,128)(2,1)S(1)}, u32[]{:S(2)}, u32[]{:S(2)}) collective-permute-start(bf16[128,512]{1,0:T(8,128)(2,1)} %get-tuple-element.107), channel_id=1, source_target_pairs={{0,2},{1,3},{2,0},{3,1},{4,6},{5,7},{6,4},{7,5},{8,10},{9,11},{10,... | collective-permute-start | bytes 393224 | tf_op jit(solution)/shard_map/ppermute | solution.py:51
  178.5 10.3 %collective-permute-done.35.refs_8_ = bf16[128,512]{1,0:T(8,128)(2,1)S(1)} collective-permute-done((bf16[128,512]{1,0:T(8,128)(2,1)}, bf16[128,512]{1,0:T(8,128)(2,1)S(1)}, u32[]{:S(2)}, u32[]{:S(2)}) %collective-permute-start.35) | collective-permute-done | bytes 131104 | tf_op jit(solution)/shard_map/ppermute | solution.py:51
  189.5 3.3 %shard_map.78 = (bf16[128,4096]{1,0:T(8,128)(2,1)}, bf16[128,2048]{1,0:T(8,128)(2,1)}, bf16[128,2048]{1,0:T(8,128)(2,1)}) custom-call(s32[2]{0:T(128)} %pad_add_fusion.place, bf16[128,512]{1,0:T(8,128)(2,1)} %get-tuple-element.72.refs_0_, bf16[128,512]{1,0:T(8,128)(2,1)} %get-tuple-element.82.refs_1_, bf16[128,512]{1,0:T(8,128)(2,1)} %get-tuple-element.92.refs_2_, ...), custom_call_target="tpu_custom_call" | custom-call | bytes 4194304 | tf_op jit(solution)/shard_map/pallas_call | solution.py:36
  (201 shorter events, 51.6 us)
Async XLA Ops:
  8.4 40.9 %collective-permute-start = (bf16[128,1024]{1,0:T(8,128)(2,1)}, bf16[128,1024]{1,0:T(8,128)(2,1)S(1)}, u32[]{:S(2)}, u32[]{:S(2)}) collective-permute-start(bf16[128,1024]{1,0:T(8,128)(2,1)} %get-tuple-element.60), channel_id=1, source_target_pairs={{0,1},{1,0},{2,3},{3,2},{4,5},{5,4},{6,7},{7,6},{8,9},{9,8},{10,11... | collective-permute-start | bytes 786440 | tf_op jit(solution)/shard_map/ppermute | solution.py:51
  8.8 41.0 %collective-permute-start.1 = (bf16[128,1024]{1,0:T(8,128)(2,1)}, bf16[128,1024]{1,0:T(8,128)(2,1)S(1)}, u32[]{:S(2)}, u32[]{:S(2)}) collective-permute-start(bf16[128,1024]{1,0:T(8,128)(2,1)} %get-tuple-element.61), channel_id=1, source_target_pairs={{0,2},{1,3},{2,0},{3,1},{4,6},{5,7},{6,4},{7,5},{8,10},{9,11},{10,... | collective-permute-start | bytes 786440 | tf_op jit(solution)/shard_map/ppermute | solution.py:51
  11.4 38.6 %collective-permute-start.2 = (bf16[128,1024]{1,0:T(8,128)(2,1)}, bf16[128,1024]{1,0:T(8,128)(2,1)S(1)}, u32[]{:S(2)}, u32[]{:S(2)}) collective-permute-start(bf16[128,1024]{1,0:T(8,128)(2,1)} %get-tuple-element.62), channel_id=1, source_target_pairs={{0,3},{1,2},{2,1},{3,0},{4,7},{5,6},{6,5},{7,4},{8,11},{9,10},{10,... | collective-permute-start | bytes 786440 | tf_op jit(solution)/shard_map/ppermute | solution.py:51
  12.7 31.6 %collective-permute-start.27 = (bf16[128,512]{1,0:T(8,128)(2,1)S(1)}, bf16[128,512]{1,0:T(8,128)(2,1)S(1)}, u32[]{:S(2)}, u32[]{:S(2)}) collective-permute-start(bf16[128,512]{1,0:T(8,128)(2,1)S(1)} %copy-done.62), channel_id=1, source_target_pairs={{0,2},{1,3},{2,0},{3,1},{4,6},{5,7},{6,4},{7,5},{8,10},{9,11},{10,... | collective-permute-start | bytes 393224 | tf_op jit(solution)/shard_map/ppermute | solution.py:51
  14.4 30.5 %collective-permute-start.28 = (bf16[128,512]{1,0:T(8,128)(2,1)S(1)}, bf16[128,512]{1,0:T(8,128)(2,1)S(1)}, u32[]{:S(2)}, u32[]{:S(2)}) collective-permute-start(bf16[128,512]{1,0:T(8,128)(2,1)S(1)} %copy-done.61), channel_id=1, source_target_pairs={{0,3},{1,2},{2,1},{3,0},{4,7},{5,6},{6,5},{7,4},{8,11},{9,10},{10,... | collective-permute-start | bytes 393224 | tf_op jit(solution)/shard_map/ppermute | solution.py:51
  50.0 20.4 %collective-permute-start.13 = (bf16[128,512]{1,0:T(8,128)(2,1)S(1)}, bf16[128,512]{1,0:T(8,128)(2,1)S(1)}, u32[]{:S(2)}, u32[]{:S(2)}) collective-permute-start(bf16[128,512]{1,0:T(8,128)(2,1)S(1)} %copy-done.48), channel_id=1, source_target_pairs={{0,2},{1,3},{2,0},{3,1},{4,6},{5,7},{6,4},{7,5},{8,10},{9,11},{10,... | collective-permute-start | bytes 393224 | tf_op jit(solution)/shard_map/ppermute | solution.py:51
  56.4 24.6 %collective-permute-start.24 = (bf16[512,256]{1,0:T(8,128)(2,1)}, bf16[512,256]{1,0:T(8,128)(2,1)S(1)}, u32[]{:S(2)}, u32[]{:S(2)}) collective-permute-start(bf16[512,256]{1,0:T(8,128)(2,1)} %get-tuple-element.93.own), channel_id=1, source_target_pairs={{0,8},{4,12},{8,16},{12,20},{16,24},{20,28},{1,9},{5,13},{9,17},{1... | collective-permute-start | bytes 786440 | tf_op jit(solution)/shard_map/ppermute | solution.py:57
  59.1 23.2 %collective-permute-start.25 = (bf16[512,256]{1,0:T(8,128)(2,1)}, bf16[512,256]{1,0:T(8,128)(2,1)S(1)}, u32[]{:S(2)}, u32[]{:S(2)}) collective-permute-start(bf16[512,256]{1,0:T(8,128)(2,1)} %get-tuple-element.93.own), channel_id=1, source_target_pairs={{0,4},{4,8},{8,12},{12,16},{16,20},{20,24},{24,28},{1,5},{5,9},{9,... | collective-permute-start | bytes 786440 | tf_op jit(solution)/shard_map/ppermute | solution.py:57
  70.5 22.7 %collective-permute-start.17 = (bf16[512,256]{1,0:T(8,128)(2,1)}, bf16[512,256]{1,0:T(8,128)(2,1)S(1)}, u32[]{:S(2)}, u32[]{:S(2)}) collective-permute-start(bf16[512,256]{1,0:T(8,128)(2,1)} %get-tuple-element.83.own), channel_id=1, source_target_pairs={{0,8},{4,12},{8,16},{12,20},{16,24},{20,28},{1,9},{5,13},{9,17},{1... | collective-permute-start | bytes 786440 | tf_op jit(solution)/shard_map/ppermute | solution.py:57
  72.2 23.0 %collective-permute-start.18 = (bf16[512,256]{1,0:T(8,128)(2,1)}, bf16[512,256]{1,0:T(8,128)(2,1)S(1)}, u32[]{:S(2)}, u32[]{:S(2)}) collective-permute-start(bf16[512,256]{1,0:T(8,128)(2,1)} %get-tuple-element.83.own), channel_id=1, source_target_pairs={{0,4},{4,8},{8,12},{12,16},{16,20},{20,24},{24,28},{1,5},{5,9},{9,... | collective-permute-start | bytes 786440 | tf_op jit(solution)/shard_map/ppermute | solution.py:57
  81.0 25.5 %collective-permute-start.10 = (bf16[512,256]{1,0:T(8,128)(2,1)}, bf16[512,256]{1,0:T(8,128)(2,1)S(1)}, u32[]{:S(2)}, u32[]{:S(2)}) collective-permute-start(bf16[512,256]{1,0:T(8,128)(2,1)} %get-tuple-element.73.own), channel_id=1, source_target_pairs={{0,8},{4,12},{8,16},{12,20},{16,24},{20,28},{1,9},{5,13},{9,17},{1... | collective-permute-start | bytes 786440 | tf_op jit(solution)/shard_map/ppermute | solution.py:57
  82.3 29.7 %collective-permute-start.11 = (bf16[512,256]{1,0:T(8,128)(2,1)}, bf16[512,256]{1,0:T(8,128)(2,1)S(1)}, u32[]{:S(2)}, u32[]{:S(2)}) collective-permute-start(bf16[512,256]{1,0:T(8,128)(2,1)} %get-tuple-element.73.own), channel_id=1, source_target_pairs={{0,4},{4,8},{8,12},{12,16},{16,20},{20,24},{24,28},{1,5},{5,9},{9,... | collective-permute-start | bytes 786440 | tf_op jit(solution)/shard_map/ppermute | solution.py:57
  91.9 29.1 %collective-permute-start.3 = (bf16[512,256]{1,0:T(8,128)(2,1)S(1)}, bf16[512,256]{1,0:T(8,128)(2,1)S(1)}, u32[]{:S(2)}, u32[]{:S(2)}) collective-permute-start(bf16[512,256]{1,0:T(8,128)(2,1)S(1)} %copy-done.23), channel_id=1, source_target_pairs={{0,8},{4,12},{8,16},{12,20},{16,24},{20,28},{1,9},{5,13},{9,17},{1... | collective-permute-start | bytes 786440 | tf_op jit(solution)/shard_map/ppermute | solution.py:57
  93.3 31.6 %collective-permute-start.4 = (bf16[512,256]{1,0:T(8,128)(2,1)S(1)}, bf16[512,256]{1,0:T(8,128)(2,1)S(1)}, u32[]{:S(2)}, u32[]{:S(2)}) collective-permute-start(bf16[512,256]{1,0:T(8,128)(2,1)S(1)} %copy-done.23), channel_id=1, source_target_pairs={{0,4},{4,8},{8,12},{12,16},{16,20},{20,24},{24,28},{1,5},{5,9},{9,... | collective-permute-start | bytes 786440 | tf_op jit(solution)/shard_map/ppermute | solution.py:57
  95.2 31.7 %collective-permute-start.29 = (bf16[512,256]{1,0:T(8,128)(2,1)}, bf16[512,256]{1,0:T(8,128)(2,1)S(1)}, u32[]{:S(2)}, u32[]{:S(2)}) collective-permute-start(bf16[512,256]{1,0:T(8,128)(2,1)} %get-tuple-element.100), channel_id=1, source_target_pairs={{4,0},{8,4},{12,8},{16,12},{20,16},{24,20},{28,24},{5,1},{9,5},{13... | collective-permute-start | bytes 786440 | tf_op jit(solution)/shard_map/ppermute | solution.py:57
  106.6 29.3 %collective-permute-start.30 = (bf16[512,256]{1,0:T(8,128)(2,1)S(1)}, bf16[512,256]{1,0:T(8,128)(2,1)S(1)}, u32[]{:S(2)}, u32[]{:S(2)}) collective-permute-start(bf16[512,256]{1,0:T(8,128)(2,1)S(1)} %copy-done.24), channel_id=1, source_target_pairs={{8,0},{12,4},{16,8},{20,12},{24,16},{28,20},{9,1},{13,5},{17,9},{2... | collective-permute-start | bytes 786440 | tf_op jit(solution)/shard_map/ppermute | solution.py:57
  112.1 25.8 %collective-permute-start.22 = (bf16[512,256]{1,0:T(8,128)(2,1)}, bf16[512,256]{1,0:T(8,128)(2,1)S(1)}, u32[]{:S(2)}, u32[]{:S(2)}) collective-permute-start(bf16[512,256]{1,0:T(8,128)(2,1)} %get-tuple-element.90), channel_id=1, source_target_pairs={{4,0},{8,4},{12,8},{16,12},{20,16},{24,20},{28,24},{5,1},{9,5},{13... | collective-permute-start | bytes 786440 | tf_op jit(solution)/shard_map/ppermute | solution.py:57
  121.1 20.9 %collective-permute-start.23 = (bf16[512,256]{1,0:T(8,128)(2,1)S(1)}, bf16[512,256]{1,0:T(8,128)(2,1)S(1)}, u32[]{:S(2)}, u32[]{:S(2)}) collective-permute-start(bf16[512,256]{1,0:T(8,128)(2,1)S(1)} %copy-done.25), channel_id=1, source_target_pairs={{8,0},{12,4},{16,8},{20,12},{24,16},{28,20},{9,1},{13,5},{17,9},{2... | collective-permute-start | bytes 786440 | tf_op jit(solution)/shard_map/ppermute | solution.py:57
  124.9 17.2 %collective-permute-start.15 = (bf16[512,256]{1,0:T(8,128)(2,1)}, bf16[512,256]{1,0:T(8,128)(2,1)S(1)}, u32[]{:S(2)}, u32[]{:S(2)}) collective-permute-start(bf16[512,256]{1,0:T(8,128)(2,1)} %get-tuple-element.80), channel_id=1, source_target_pairs={{4,0},{8,4},{12,8},{16,12},{20,16},{24,20},{28,24},{5,1},{9,5},{13... | collective-permute-start | bytes 786440 | tf_op jit(solution)/shard_map/ppermute | solution.py:57
  126.9 20.5 %collective-permute-start.16 = (bf16[512,256]{1,0:T(8,128)(2,1)}, bf16[512,256]{1,0:T(8,128)(2,1)S(1)}, u32[]{:S(2)}, u32[]{:S(2)}) collective-permute-start(bf16[512,256]{1,0:T(8,128)(2,1)} %get-tuple-element.81), channel_id=1, source_target_pairs={{8,0},{12,4},{16,8},{20,12},{24,16},{28,20},{9,1},{13,5},{17,9},{2... | collective-permute-start | bytes 786440 | tf_op jit(solution)/shard_map/ppermute | solution.py:57
  151.1 19.4 %collective-permute-start.37 = (bf16[128,512]{1,0:T(8,128)(2,1)S(1)}, bf16[128,512]{1,0:T(8,128)(2,1)S(1)}, u32[]{:S(2)}, u32[]{:S(2)}) collective-permute-start(bf16[128,512]{1,0:T(8,128)(2,1)S(1)} %copy-done.59), channel_id=1, source_target_pairs={{0,2},{1,3},{2,0},{3,1},{4,6},{5,7},{6,4},{7,5},{8,10},{9,11},{10,... | collective-permute-start | bytes 393224 | tf_op jit(solution)/shard_map/ppermute | solution.py:51
  155.6 21.1 %collective-permute-start.32 = (bf16[128,512]{1,0:T(8,128)(2,1)}, bf16[128,512]{1,0:T(8,128)(2,1)S(1)}, u32[]{:S(2)}, u32[]{:S(2)}) collective-permute-start(bf16[128,512]{1,0:T(8,128)(2,1)} %get-tuple-element.104), channel_id=1, source_target_pairs={{0,1},{1,0},{2,3},{3,2},{4,5},{5,4},{6,7},{7,6},{8,9},{9,8},{10,11... | collective-permute-start | bytes 393224 | tf_op jit(solution)/shard_map/ppermute | solution.py:51
  157.9 19.7 %collective-permute-start.36 = (bf16[128,512]{1,0:T(8,128)(2,1)S(1)}, bf16[128,512]{1,0:T(8,128)(2,1)S(1)}, u32[]{:S(2)}, u32[]{:S(2)}) collective-permute-start(bf16[128,512]{1,0:T(8,128)(2,1)S(1)} %copy-done.58), channel_id=1, source_target_pairs={{0,2},{1,3},{2,0},{3,1},{4,6},{5,7},{6,4},{7,5},{8,10},{9,11},{10,... | collective-permute-start | bytes 393224 | tf_op jit(solution)/shard_map/ppermute | solution.py:51
  170.6 18.2 %collective-permute-start.35 = (bf16[128,512]{1,0:T(8,128)(2,1)}, bf16[128,512]{1,0:T(8,128)(2,1)S(1)}, u32[]{:S(2)}, u32[]{:S(2)}) collective-permute-start(bf16[128,512]{1,0:T(8,128)(2,1)} %get-tuple-element.107), channel_id=1, source_target_pairs={{0,2},{1,3},{2,0},{3,1},{4,6},{5,7},{6,4},{7,5},{8,10},{9,11},{10,... | collective-permute-start | bytes 393224 | tf_op jit(solution)/shard_map/ppermute | solution.py:51
  (82 other events, 1060.0 us)
where the time goes:
time: 195 us; the launch traced here: 193 us
  starting transfers between devices  86 us (44%)
  waiting for transfers between devices  55.7 us (29%)
  Pallas kernels  47.3 us (24%)
    ppermute x27, waiting for transfers between devices, across(): return lax.ppermute(shard, 'head', [(i, i ^ step) for i in range(parts)])  55.7 us
    ppermute x27, starting transfers between devices, across(): return lax.ppermute(shard, 'head', [(i, i ^ step) for i in range(parts)])  49.5 us
    pallas_call x12, Pallas kernels, local_call(): pl.pallas_call(body, out_shape=outs, in_specs=[smem()] + [vmem()] * (len(...  47.3 us
    ppermute x16, starting transfers between devices, shifted(): return lax.ppermute(shard, 'ctx', pairs)  36.6 us
  transfers between devices with their start and end apart: 43, of which 8 were waited for; matrix products, arithmetic and copies ran while one was open for 0% of the time, Pallas kernels for 21%

commit v1 on v0

v1 whole, which is shorter than its diff:
```python
import functools

import jax
import jax.numpy as jnp
from jax import lax
from jax.experimental import pallas as pl
from jax.experimental.pallas import tpu as pltpu
from jax.sharding import PartitionSpec as P


HEAD_DIM = 128
Q_HEADS = 32
KV_HEADS = 16
WINDOW = 1024
GROUPS = Q_HEADS // KV_HEADS
Q_COLS = GROUPS * HEAD_DIM
TILE = 128

score_scale = 168.0 ** (-0.5)
LOG2_E = 1.4426950408889634


def vmem():
    return pl.BlockSpec(memory_space=pltpu.VMEM)


def smem():
    return pl.BlockSpec(memory_space=pltpu.SMEM)


def moved_bytes(arrays):
    return sum(a.size * a.dtype.itemsize for a in arrays)


def local_call(body, outs, args, flops=0, transcendentals=0, scratch=()):
    return pl.pallas_call(
        body,
        out_shape=outs,
        in_specs=[smem()] + [vmem()] * (len(args) - 1),
        out_specs=[vmem()] * len(outs),
        scratch_shapes=list(scratch),
        cost_estimate=pl.CostEstimate(
            flops=flops,
            transcendentals=transcendentals,
            bytes_accessed=moved_bytes(list(args[1:]) + list(outs)),
        ),
    )(*args)


def sent_to(place, step, parts):
    if parts == 4 and step in (1, 3):
        return lax.rem(2 * place + 1 if step == 1 else 3 * place + 2, 5)
    if parts == 4 and step == 2:
        step = 3
    return jnp.bitwise_xor(place, step)


def came_from(place, step, parts):
    return sent_to(place, (parts - step) % parts if parts == 4 else step, parts)


def across(shard, parts, step):
    if parts == 4:
        moves = list(enumerate({1: (1, 3, 0, 2), 2: (3, 2, 1, 0), 3: (2, 0, 3, 1)}[step]))
    else:
        moves = [(i, i ^ step) for i in range(parts)]
    return lax.ppermute(shard, "head", moves)


def pack_two(parts, width, chunks, place, left, right, *outs):
    for step in range(parts):
        partner = sent_to(place[0], step, parts)
        for chunk in range(chunks):
            out = outs[step * chunks + chunk]
            start = pl.multiple_of((partner * chunks + chunk) * width, width)
            out[:, 0:width] = left[:, pl.ds(start, width)]
            out[:, width : 2 * width] = right[:, pl.ds(start, width)]


def split_rows(parts, pairs, width, place, *refs):
    outs = refs[parts:]
    rows = refs[0].shape[0]
    for step in range(parts):
        partner = came_from(place[0], step, parts)
        at = pl.ds(pl.multiple_of(partner * rows, rows), rows)
        for pair in range(pairs):
            for other in range(len(outs) // pairs):
                core = jnp.bitwise_xor(place[2], other)
                for side in range(2):
                    start = ((side * pairs + pair) * place[3] + core) * width
                    outs[other * pairs + pair][at, side * width : (side + 1) * width] = refs[step][
                        :, pl.ds(pl.multiple_of(start, width), width)
                    ]


def attend(kv_count, q_count, starts, place, *refs):
    kv_refs = refs[:kv_count]
    q_refs = refs[kv_count : kv_count + q_count]
    dq_outs = refs[kv_count + q_count : kv_count + 2 * q_count]
    kv_outs = refs[kv_count + 2 * q_count : 2 * kv_count + 2 * q_count]
    scratch = refs[2 * kv_count + 2 * q_count :]
    q_rows, g_rows, keys, values, keys_t, score, d_att, att_low, d_low, dk, dv, dq_all = scratch
    block = q_refs[0].shape[0]
    span = score.shape[0]
    tiles = span // TILE
    places = [pl.ds(pl.multiple_of(at, TILE), block) for at in starts(place, block)]
    for at, q in zip(places[kv_count:], q_refs):
        q_rows[at, :] = q[:, 0:Q_COLS]
        g_rows[at, :] = q[:, Q_COLS : 2 * Q_COLS]
    for at, kv in zip(places, kv_refs):
        keys[at, :] = kv[:, 0:HEAD_DIM]
        values[at, :] = kv[:, HEAD_DIM : 2 * HEAD_DIM]
        keys_t[:, at] = kv[:, 0:HEAD_DIM].T
    dk[...] = jnp.zeros_like(dk)
    dv[...] = jnp.zeros_like(dv)
    first_key = WINDOW - place[1] * (q_count * block)
    lanes = GROUPS * TILE
    key_id = lax.broadcasted_iota(jnp.int32, (TILE, lanes), 0)
    row_id = jnp.bitwise_and(lax.broadcasted_iota(jnp.int32, (TILE, lanes), 1), TILE - 1)
    lower = key_id <= row_id
    across_cols = (((1,), (1,)), ((), ()))
    exponent = jnp.float32(score_scale * LOG2_E)

    def fold(x):
        return x.reshape(TILE // 8, 8, lanes)

    for row_block in range(q_count * block // TILE):
        base = row_block * TILE
        these = slice(base, base + TILE)
        q_two = jnp.concatenate(
            [q_rows[these, g * HEAD_DIM : (g + 1) * HEAD_DIM] for g in range(GROUPS)], axis=0
        )
        g_two = jnp.concatenate(
            [g_rows[these, g * HEAD_DIM : (g + 1) * HEAD_DIM] for g in range(GROUPS)], axis=0
        )
        there = slice(base, base + span)
        score[...] = lax.dot_general(
            keys[there, :], q_two, across_cols, preferred_element_type=jnp.float32
        )
        d_att[...] = lax.dot_general(
            values[there, :], g_two, across_cols, preferred_element_type=jnp.float32
        )
        score[0:TILE, :] = jnp.where(lower, -1e30, score[0:TILE, :])
        score[span - TILE : span, :] = jnp.where(lower, score[span - TILE : span, :], -1e30)
        top = jnp.full((8, lanes), -1e30, jnp.float32)
        for t in range(tiles):
            s = score[t * TILE : (t + 1) * TILE, :]
            gone = jnp.where(base + t * TILE < first_key, -1e30, 0.0)
            top = jnp.maximum(top, jnp.max(fold(s), axis=0) + gone)
        top = jnp.max(top, axis=0, keepdims=True)
        total = jnp.zeros((8, lanes), jnp.float32)
        inner = jnp.zeros((8, lanes), jnp.float32)
        for t in range(tiles):
            here = slice(t * TILE, (t + 1) * TILE)
            level = top + jnp.where(base + t * TILE < first_key, 1e30, 0.0)
            p = jnp.exp2((score[here, :] - level) * exponent)
            score[here, :] = p
            total = total + jnp.sum(fold(p), axis=0)
            inner = inner + jnp.sum(fold(p * d_att[here, :]), axis=0)
        inverse = 1.0 / jnp.sum(total, axis=0, keepdims=True)
        center = jnp.sum(inner, axis=0, keepdims=True) * inverse
        for t in range(tiles):
            here = slice(t * TILE, (t + 1) * TILE)
            att = score[here, :] * inverse
            att_low[here, :] = att.astype(jnp.bfloat16)
            d_low[here, :] = (att * (d_att[here, :] - center)).astype(jnp.bfloat16)
        dv[there, :] += jnp.dot(att_low[...], g_two, preferred_element_type=jnp.float32)
        dk[there, :] += jnp.dot(d_low[...], q_two, preferred_element_type=jnp.float32)
        dq_t = jnp.dot(keys_t[:, there], d_low[...], preferred_element_type=jnp.float32)
        dq = (dq_t * score_scale).T.astype(jnp.bfloat16)
        for g in range(GROUPS):
            dq_all[these, g * HEAD_DIM : (g + 1) * HEAD_DIM] = dq[g * TILE : (g + 1) * TILE, :]
    for at, out in zip(places[kv_count:], dq_outs):
        out[...] = dq_all[at, :]
    for at, out in zip(places, kv_outs):
        out[:, 0:HEAD_DIM] = (dk[at, :] * score_scale).astype(out.dtype)
        out[:, HEAD_DIM : 2 * HEAD_DIM] = dv[at, :].astype(out.dtype)


def row_starts_single(place, block):
    return [0, block, 2 * block, 0]


def row_starts_pair(place, block):
    here, there = place[2] * block, (1 - place[2]) * block
    return [here, there, 2 * block + here, 2 * block + there, here, there]


def cut_queries(parts, place, kept, given, *outs):
    rows = outs[0].shape[0]
    width = kept.shape[1]
    for step in range(parts):
        at = pl.ds(pl.multiple_of(sent_to(place[0], step, parts) * rows, rows), rows)
        for other, source in enumerate((kept, given)):
            core = jnp.bitwise_xor(place[2], other)
            outs[step][:, pl.ds(pl.multiple_of(core * width, width), width)] = source[at, :]


def cut_keys(parts, place, own, own_far, given, given_far, *outs):
    rows = outs[0].shape[0]
    for step in range(parts):
        at = pl.ds(pl.multiple_of(sent_to(place[0], step, parts) * rows, rows), rows)
        for other, (one, two) in enumerate(((own, own_far), (given, given_far))):
            core = jnp.bitwise_xor(place[2], other)
            total = (one[at, :].astype(jnp.float32) + two[at, :].astype(jnp.float32)).astype(
                jnp.bfloat16
            )
            for side in range(2):
                start = pl.multiple_of((2 * side + core) * HEAD_DIM, HEAD_DIM)
                outs[step][:, pl.ds(start, HEAD_DIM)] = total[
                    :, side * HEAD_DIM : (side + 1) * HEAD_DIM
                ]


def add_up(parts, place, dq, own, near, far, *outs):
    rows = outs[0].shape[0]
    for step in range(parts):
        partner = sent_to(place[0], step, parts)
        at = pl.ds(pl.multiple_of(partner * rows, rows), rows)
        outs[step][:, 0:Q_COLS] = dq[at, :]
        total = own[at, :] + near[at, :].astype(jnp.float32) + far[at, :].astype(jnp.float32)
        outs[parts + step][:, 0 : 2 * HEAD_DIM] = total.astype(jnp.bfloat16)


def unpack(parts, chunks, width, place, *refs):
    pieces = refs[: parts * chunks]
    outs = refs[parts * chunks :]
    for step in range(parts):
        partner = came_from(place[0], step, parts)
        for chunk in range(chunks):
            piece = pieces[step * chunks + chunk]
            start = pl.multiple_of((partner * chunks + chunk) * width, width)
            for i, out in enumerate(outs):
                out[:, pl.ds(start, width)] = piece[:, i * width : (i + 1) * width]


def struct(shape, dtype=jnp.bfloat16):
    return jax.ShapeDtypeStruct(shape, dtype)


def to_partners(pieces, parts):
    return [pieces[0]] + [across(pieces[s], parts, s) for s in range(1, parts)]


def ctx_moved(shard, by, flip):
    count = lax.axis_size("ctx")
    moves = [(i, (i + by) ^ flip) for i in range(count) if 0 <= i + by < count]
    return lax.ppermute(shard, "ctx", moves)


def attend_call(starts, kv, q, kv_dtypes, place):
    block = q[0].shape[0]
    rows, key_count, span = len(q) * block, len(kv) * block, WINDOW + TILE
    lanes = GROUPS * TILE
    pairs = rows * span * GROUPS
    low, wide = jnp.bfloat16, jnp.float32
    outs = [struct((block, Q_COLS))] * len(q) + [
        struct((block, 2 * HEAD_DIM), dtype) for dtype in kv_dtypes
    ]
    result = functools.partial(
        local_call,
        flops=10 * pairs * HEAD_DIM,
        transcendentals=pairs,
        scratch=[
            pltpu.VMEM((rows, Q_COLS), low),
            pltpu.VMEM((rows, Q_COLS), low),
            pltpu.VMEM((key_count, HEAD_DIM), low),
            pltpu.VMEM((key_count, HEAD_DIM), low),
            pltpu.VMEM((HEAD_DIM, key_count), low),
            pltpu.VMEM((span, lanes), wide),
            pltpu.VMEM((span, lanes), wide),
            pltpu.VMEM((span, lanes), low),
            pltpu.VMEM((span, lanes), low),
            pltpu.VMEM((key_count, HEAD_DIM), wide),
            pltpu.VMEM((key_count, HEAD_DIM), wide),
            pltpu.VMEM((rows, Q_COLS), low),
        ],
    )(functools.partial(attend, len(kv), len(q), starts), outs, (place, *kv, *q))
    return result[: len(q)], result[len(q) :]


def shards(queries, key_rows, value_rows, out_grad):
    parts = lax.axis_size("head")
    rows = queries.shape[0]
    block = rows * parts
    heads = KV_HEADS // parts
    cores = 2 if heads % 2 == 0 else 1
    chunks = heads // cores
    ctx = lax.axis_index("ctx")
    place = jnp.stack(
        [lax.axis_index("head"), ctx // cores, ctx % cores, jnp.int32(cores)]
    ).astype(jnp.int32)

    kv_pieces = local_call(
        functools.partial(pack_two, parts, heads * HEAD_DIM, 1),
        [struct((rows, 2 * heads * HEAD_DIM))] * parts,
        (place, key_rows, value_rows),
    )
    kv_pieces = to_partners(kv_pieces, parts)
    q_piece = struct((rows, 2 * cores * Q_COLS))
    q_pieces = local_call(
        functools.partial(pack_two, parts, cores * Q_COLS, chunks),
        [q_piece] * (parts * chunks),
        (place, queries, out_grad),
    )
    arrived = [to_partners(q_pieces[c::chunks], parts) for c in range(chunks)]
    kv_split = local_call(
        functools.partial(split_rows, parts, chunks, HEAD_DIM),
        [struct((block, 2 * HEAD_DIM))] * (cores * chunks),
        (place, *kv_pieces),
    )
    halos = []
    for chunk in range(chunks):
        keep = kv_split[chunk]
        if cores == 2:
            give = kv_split[chunks + chunk]
            halos.append(
                (ctx_moved(keep, 2, 0), ctx_moved(give, 2, 1), keep, ctx_moved(give, 0, 1))
            )
        else:
            halos.append((ctx_moved(keep, 2, 0), ctx_moved(keep, 1, 0), keep))
    dq_back, kv_back = [], []
    for chunk in range(chunks):
        q_split = local_call(
            functools.partial(split_rows, parts, 1, Q_COLS),
            [struct((block, 2 * Q_COLS))] * cores,
            (place, *arrived[chunk]),
        )
        kv_piece = struct((rows, cores * 2 * HEAD_DIM))
        dq_piece = struct((rows, cores * Q_COLS))
        low, wide = jnp.bfloat16, jnp.float32
        if cores == 2:
            q_here = [q_split[0], ctx_moved(q_split[1], 0, 1)]
            (dq_keep, dq_give), (far_a, far_b, own, give) = attend_call(
                row_starts_pair, halos[chunk], q_here, (low, low, wide, low), place
            )
            dq_got = ctx_moved(dq_give, 0, 1)
            far_a = ctx_moved(far_a, -2, 0)
            far_b = ctx_moved(far_b, -2, 1)
            got = ctx_moved(give, 0, 1)
            dq_sent = local_call(
                functools.partial(cut_queries, parts), [dq_piece] * parts, (place, dq_keep, dq_got)
            )
            kv_sent = local_call(
                functools.partial(cut_keys, parts),
                [kv_piece] * parts,
                (place, own, far_a, got, far_b),
            )
        else:
            (dq_keep,), (far, near, own) = attend_call(
                row_starts_single, halos[chunk], q_split, (low, low, wide), place
            )
            far = ctx_moved(far, -2, 0)
            near = ctx_moved(near, -1, 0)
            sent = local_call(
                functools.partial(add_up, parts),
                [dq_piece] * parts + [kv_piece] * parts,
                (place, dq_keep, own, near, far),
            )
            dq_sent, kv_sent = sent[:parts], sent[parts:]
        dq_back.append(to_partners(dq_sent, parts))
        kv_back.append(to_partners(kv_sent, parts))
    (query_grad,) = local_call(
        functools.partial(unpack, parts, chunks, cores * Q_COLS),
        [struct(queries.shape)],
        (place, *[dq_back[c][s] for s in range(parts) for c in range(chunks)]),
    )
    key_grad, value_grad = local_call(
        functools.partial(unpack, parts, chunks, cores * HEAD_DIM),
        [struct(key_rows.shape), struct(value_rows.shape)],
        (place, *[kv_back[c][s] for s in range(parts) for c in range(chunks)]),
    )
    return query_grad, key_grad, value_grad


def solution(mesh):
    spec = P(("ctx", "head"), None)
    return jax.shard_map(
        shards,
        mesh=mesh,
        in_specs=(spec, spec, spec, spec),
        out_specs=(spec, spec, spec),
        check_vma=False,
    )
```

time: 195 us -> 181 us (0.928)
  waiting for transfers between devices: 55.7 us -> 26.5 us
  starting transfers between devices: 86 us -> 94 us
  local copies, waits for them, and re-layouts: 1.53 us -> 5.72 us
  Pallas kernels: 47.3 us -> 49.9 us
    ppermute x43 -> x37, waiting for transfers between devices: 55.7 us -> 26.5 us  [the longest x21 21.3 us: across(): return lax.ppermute(shard, 'head', moves)]
    ppermute x43 -> x37, starting transfers between devices: 86 us -> 94 us  [the longest x21 74.3 us: across(): return lax.ppermute(shard, 'head', moves)]
    unnamed x126 -> x94, local copies, waits for them, and re-layouts: 1.53 us -> 5.72 us
    pallas_call x12 -> x13, Pallas kernels: 47.3 us -> 49.9 us  [local_call(): pl.pallas_call(body, out_shape=outs, in_specs=[smem()] + [vmem()] * (len(...]
  transfers between devices with their start and end apart: 43 -> 37, of which waited for: 8 -> 8; matrix products, arithmetic and copies ran while one was open for 0% -> 0% of each run, Pallas kernels for 21% -> 25%
where the time goes in v1:
time: 181 us; the launch traced here: 178 us
  starting transfers between devices  94 us (52%)
  Pallas kernels  49.9 us (28%)
  waiting for transfers between devices  26.5 us (15%)
  local copies, waits for them, and re-layouts  5.72 us (3%)
    ppermute x21, starting transfers between devices, across(): return lax.ppermute(shard, 'head', moves)  74.3 us
    pallas_call x13, Pallas kernels, local_call(): pl.pallas_call(body, out_shape=outs, in_specs=[smem()] + [vmem()] * (len(...  49.9 us
    ppermute x21, waiting for transfers between devices, across(): return lax.ppermute(shard, 'head', moves)  21.3 us
    ppermute x16, starting transfers between devices, ctx_moved(): return lax.ppermute(shard, 'ctx', moves)  19.7 us
    unnamed x94, local copies, waits for them, and re-layouts  5.72 us
    ppermute x16, waiting for transfers between devices, ctx_moved(): return lax.ppermute(shard, 'ctx', moves)  5.19 us
  transfers between devices with their start and end apart: 37, of which 8 were waited for; matrix products, arithmetic and copies ran while one was open for 0% of the time, Pallas kernels for 25%

profile of v1, /device:TPU:6, one launch (start us, length us, event | category | flops | bytes accessed | tf_op | source)
XLA Modules:
  0.0 177.9 jit_solution(8675768152622924147)
XLA Ops:
  1.3 3.0 %shard_map.69 = (bf16[128,1024]{1,0:T(8,128)(2,1)}, bf16[128,1024]{1,0:T(8,128)(2,1)}, bf16[128,1024]{1,0:T(8,128)(2,1)}, bf16[128,1024]{1,0:T(8,128)(2,1)}, bf1...) custom-call(s32[4]{0:T(128)} %pad_add_fusion.place, ...), custom_call_target="tpu_custom_call" | custom-call | bytes 4194304 | tf_op jit(solution)/shard_map/pallas_call | solution.py:36
  5.9 2.5 %collective-permute-start.15 = (bf16[128,1024]{1,0:T(8,128)(2,1)}, bf16[128,1024]{1,0:T(8,128)(2,1)S(1)}, u32[]{:S(2)}, u32[]{:S(2)}) collective-permute-start(bf16[128,1024]{1,0:T(8,128)(2,1)} %get-tuple-element.72), channel_id=1, source_target_pairs={{0,3},{1,2},{2,1},{3,0},{4,7},{5,6},{6,5},{7,4},{8,11},{9,10},{10,... | collective-permute-start | bytes 786440 | tf_op jit(solution)/shard_map/ppermute | solution.py:67
  10.0 2.3 %shard_map.67 = (bf16[128,1024]{1,0:T(8,128)(2,1)}, bf16[128,1024]{1,0:T(8,128)(2,1)}, bf16[128,1024]{1,0:T(8,128)(2,1)}, bf16[128,1024]{1,0:T(8,128)(2,1)}) custom-call(s32[4]{0:T(128)} %pad_add_fusion.place, bf16[128,2048]{1,0:T(8,128)(2,1)} %left.2, bf16[128,2048]{1,0:T(8,128)(2,1)} %right.2), custom_call_target="tpu_custom_call" | custom-call | bytes 2097152 | tf_op jit(solution)/shard_map/pallas_call | solution.py:36
  16.3 5.2 %collective-permute-done.15.refs_2_ = bf16[128,1024]{1,0:T(8,128)(2,1)S(1)} collective-permute-done((bf16[128,1024]{1,0:T(8,128)(2,1)}, bf16[128,1024]{1,0:T(8,128)(2,1)S(1)}, u32[]{:S(2)}, u32[]{:S(2)}) %collective-permute-start.15) | collective-permute-done | bytes 262176 | tf_op jit(solution)/shard_map/ppermute | solution.py:67
  21.5 22.2 %collective-permute-start.6 = (bf16[128,1024]{1,0:T(8,128)(2,1)S(1)}, bf16[128,1024]{1,0:T(8,128)(2,1)S(1)}, u32[]{:S(2)}, u32[]{:S(2)}) collective-permute-start(bf16[128,1024]{1,0:T(8,128)(2,1)S(1)} %copy-done.36), channel_id=1, source_target_pairs={{0,1},{1,3},{2,0},{3,2},{4,5},{5,7},{6,4},{7,6},{8,9},{9,11},{10,8... | collective-permute-start | bytes 786440 | tf_op jit(solution)/shard_map/ppermute | solution.py:67
  43.7 3.3 %collective-permute-start.7 = (bf16[128,1024]{1,0:T(8,128)(2,1)S(1)}, bf16[128,1024]{1,0:T(8,128)(2,1)S(1)}, u32[]{:S(2)}, u32[]{:S(2)}) collective-permute-start(bf16[128,1024]{1,0:T(8,128)(2,1)S(1)} %copy-done.34), channel_id=1, source_target_pairs={{0,3},{1,2},{2,1},{3,0},{4,7},{5,6},{6,5},{7,4},{8,11},{9,10},{10,... | collective-permute-start | bytes 786440 | tf_op jit(solution)/shard_map/ppermute | solution.py:67
  47.0 2.4 %shard_map.73 = (bf16[512,512]{1,0:T(8,128)(2,1)}, bf16[512,512]{1,0:T(8,128)(2,1)}) custom-call(s32[4]{0:T(128)} %pad_add_fusion.place, bf16[128,1024]{1,0:T(8,128)(2,1)} %get-tuple-element.70.refs_0_, bf16[128,1024]{1,0:T(8,128)(2,1)} %copy-done.13, bf16[128,1024]{1,0:T(8,128)(2,1)} %copy-done.14, bf16[128,1024]{1,0:T(8,128)(2,1)} %copy-done.16), custom_call_target="tpu_custom_call" | custom-call | bytes 2097152 | tf_op jit(solution)/shard_map/pallas_call | solution.py:36
  51.2 11.1 %collective-permute-start.8 = (bf16[128,1024]{1,0:T(8,128)(2,1)S(1)}, bf16[128,1024]{1,0:T(8,128)(2,1)S(1)}, u32[]{:S(2)}, u32[]{:S(2)}) collective-permute-start(bf16[128,1024]{1,0:T(8,128)(2,1)S(1)} %copy-done.33), channel_id=1, source_target_pairs={{0,2},{1,0},{2,3},{3,1},{4,6},{5,4},{6,7},{7,5},{8,10},{9,8},{10,1... | collective-permute-start | bytes 786440 | tf_op jit(solution)/shard_map/ppermute | solution.py:67
  63.0 2.4 %shard_map.68 = (bf16[512,256]{1,0:T(8,128)(2,1)}, bf16[512,256]{1,0:T(8,128)(2,1)}, bf16[512,256]{1,0:T(8,128)(2,1)}, bf16[512,256]{1,0:T(8,128)(2,1)}) custom-call(s32[4]{0:T(128)} %pad_add_fusion.place, bf16[128,1024]{1,0:T(8,128)(2,1)} %get-tuple-element.53.refs_0_, bf16[128,1024]{1,0:T(8,128)(2,1)} %copy-done.10, bf16[128,1024]{1,0:T(8,128)(2,1)} %copy-done.11, ...), custom_call_target="tpu_custom_call" | custom-call | bytes 2097152 | tf_op jit(solution)/shard_map/pallas_call | solution.py:36
  66.7 4.2 %collective-permute-done.6.refs_1_ = bf16[128,1024]{1,0:T(8,128)(2,1)S(1)} collective-permute-done((bf16[128,1024]{1,0:T(8,128)(2,1)S(1)}, bf16[128,1024]{1,0:T(8,128)(2,1)S(1)}, u32[]{:S(2)}, u32[]{:S(2)}) %collective-permute-start.6) | collective-permute-done | bytes 262176 | tf_op jit(solution)/shard_map/ppermute | solution.py:67
  73.0 2.4 %shard_map.70 = (bf16[512,512]{1,0:T(8,128)(2,1)}, bf16[512,512]{1,0:T(8,128)(2,1)}) custom-call(s32[4]{0:T(128)} %pad_add_fusion.place, bf16[128,1024]{1,0:T(8,128)(2,1)} %get-tuple-element.59.refs_0_, bf16[128,1024]{1,0:T(8,128)(2,1)} %copy-done.8, bf16[128,1024]{1,0:T(8,128)(2,1)} %copy-done.9, bf16[128,1024]{1,0:T(8,128)(2,1)} %copy-done.15), custom_call_target="tpu_custom_call" | custom-call | bytes 2097152 | tf_op jit(solution)/shard_map/pallas_call | solution.py:36
  77.2 3.5 %collective-permute-done.12.refs_1_ = bf16[512,256]{1,0:T(8,128)(2,1)S(1)} collective-permute-done((bf16[512,256]{1,0:T(8,128)(2,1)}, bf16[512,256]{1,0:T(8,128)(2,1)S(1)}, u32[]{:S(2)}, u32[]{:S(2)}) %collective-permute-start.12) | collective-permute-done | bytes 262176 | tf_op jit(solution)/shard_map/ppermute | solution.py:248
  83.8 12.3 %shard_map.74 = (bf16[512,256]{1,0:T(8,128)(2,1)}, bf16[512,256]{1,0:T(8,128)(2,1)}, bf16[512,256]{1,0:T(8,128)(2,1)}, bf16[512,256]{1,0:T(8,128)(2,1)}, f32[512,256]{1,0:T(8,128)}, /*index=5*/bf16[512,256]{1,0:T(8,128)(2,1)}) custom-call(s32[4]{0:T(128)} %pad_add_fusion.place, bf16[512,256]{1,0:T(8,128)(2,1)} %copy-done.38, bf16[512,256]{1,0:T(8,128)(2,1)} %copy-done.40, ...), custom_call_target="tpu_custom_call" | custom-call | flops 3019898880 | bytes 3932160 | tf_op jit(solution)/shard_map/pallas_call | solution.py:36
  96.1 4.6 %collective-permute-start.28 = (bf16[512,256]{1,0:T(8,128)(2,1)}, bf16[512,256]{1,0:T(8,128)(2,1)S(1)}, u32[]{:S(2)}, u32[]{:S(2)}) collective-permute-start(bf16[512,256]{1,0:T(8,128)(2,1)} %get-tuple-element.91), channel_id=1, source_target_pairs={{8,0},{12,4},{16,8},{20,12},{24,16},{28,20},{9,1},{13,5},{17,9},{2... | collective-permute-start | bytes 786440 | tf_op jit(solution)/shard_map/ppermute | solution.py:248
  100.7 4.5 %collective-permute-start.30 = (bf16[512,256]{1,0:T(8,128)(2,1)}, bf16[512,256]{1,0:T(8,128)(2,1)S(1)}, u32[]{:S(2)}, u32[]{:S(2)}) collective-permute-start(bf16[512,256]{1,0:T(8,128)(2,1)} %get-tuple-element.93), channel_id=1, source_target_pairs={{8,4},{12,0},{16,12},{20,8},{24,20},{28,16},{9,5},{13,1},{17,13},{... | collective-permute-start | bytes 786440 | tf_op jit(solution)/shard_map/ppermute | solution.py:248
  106.2 12.3 %shard_map.71 = (bf16[512,256]{1,0:T(8,128)(2,1)}, bf16[512,256]{1,0:T(8,128)(2,1)}, bf16[512,256]{1,0:T(8,128)(2,1)}, bf16[512,256]{1,0:T(8,128)(2,1)}, f32[512,256]{1,0:T(8,128)}, /*index=5*/bf16[512,256]{1,0:T(8,128)(2,1)}) custom-call(s32[4]{0:T(128)} %pad_add_fusion.place, bf16[512,256]{1,0:T(8,128)(2,1)} %copy-done.41, bf16[512,256]{1,0:T(8,128)(2,1)} %copy-done.37, ...), custom_call_target="tpu_custom_call" | custom-call | flops 3019898880 | bytes 3932160 | tf_op jit(solution)/shard_map/pallas_call | solution.py:36
  129.7 3.4 %collective-permute-start.34 = (bf16[128,512]{1,0:T(8,128)(2,1)}, bf16[128,512]{1,0:T(8,128)(2,1)S(1)}, u32[]{:S(2)}, u32[]{:S(2)}) collective-permute-start(bf16[128,512]{1,0:T(8,128)(2,1)} %get-tuple-element.98), channel_id=1, source_target_pairs={{0,3},{1,2},{2,1},{3,0},{4,7},{5,6},{6,5},{7,4},{8,11},{9,10},{10,... | collective-permute-start | bytes 393224 | tf_op jit(solution)/shard_map/ppermute | solution.py:67
  133.1 3.2 %collective-permute-start.36 = (bf16[128,512]{1,0:T(8,128)(2,1)}, bf16[128,512]{1,0:T(8,128)(2,1)S(1)}, u32[]{:S(2)}, u32[]{:S(2)}) collective-permute-start(bf16[128,512]{1,0:T(8,128)(2,1)} %get-tuple-element.100), channel_id=1, source_target_pairs={{0,2},{1,0},{2,3},{3,1},{4,6},{5,4},{6,7},{7,5},{8,10},{9,8},{10,1... | collective-permute-start | bytes 393224 | tf_op jit(solution)/shard_map/ppermute | solution.py:67
  146.7 6.4 %collective-permute-start.22 = (bf16[128,512]{1,0:T(8,128)(2,1)S(1)}, bf16[128,512]{1,0:T(8,128)(2,1)S(1)}, u32[]{:S(2)}, u32[]{:S(2)}) collective-permute-start(bf16[128,512]{1,0:T(8,128)(2,1)S(1)} %copy-done.44), channel_id=1, source_target_pairs={{0,3},{1,2},{2,1},{3,0},{4,7},{5,6},{6,5},{7,4},{8,11},{9,10},{10,... | collective-permute-start | bytes 393224 | tf_op jit(solution)/shard_map/ppermute | solution.py:67
  154.5 7.3 %collective-permute-start.19 = (bf16[128,512]{1,0:T(8,128)(2,1)}, bf16[128,512]{1,0:T(8,128)(2,1)S(1)}, u32[]{:S(2)}, u32[]{:S(2)}) collective-permute-start(bf16[128,512]{1,0:T(8,128)(2,1)} %get-tuple-element.79), channel_id=1, source_target_pairs={{0,1},{1,3},{2,0},{3,2},{4,5},{5,7},{6,4},{7,6},{8,9},{9,11},{10,8... | collective-permute-start | bytes 393224 | tf_op jit(solution)/shard_map/ppermute | solution.py:67
  161.8 3.5 %collective-permute-start.21 = (bf16[128,512]{1,0:T(8,128)(2,1)}, bf16[128,512]{1,0:T(8,128)(2,1)S(1)}, u32[]{:S(2)}, u32[]{:S(2)}) collective-permute-start(bf16[128,512]{1,0:T(8,128)(2,1)} %get-tuple-element.81), channel_id=1, source_target_pairs={{0,3},{1,2},{2,1},{3,0},{4,7},{5,6},{6,5},{7,4},{8,11},{9,10},{10,... | collective-permute-start | bytes 393224 | tf_op jit(solution)/shard_map/ppermute | solution.py:67
  165.4 2.4 %shard_map.79 = (bf16[128,2048]{1,0:T(8,128)(2,1)}, bf16[128,2048]{1,0:T(8,128)(2,1)}) custom-call(s32[4]{0:T(128)} %pad_add_fusion.place, bf16[128,512]{1,0:T(8,128)(2,1)} %get-tuple-element.89.refs_0_, bf16[128,512]{1,0:T(8,128)(2,1)} %get-tuple-element.94.refs_1_, bf16[128,512]{1,0:T(8,128)(2,1)} %copy-done.26, bf16[128,512]{1,0:T(8,128)(2,1)} %copy-done.23, ...), custom_call_target="tpu_custom_call" | custom-call | bytes 2097152 | tf_op jit(solution)/shard_map/pallas_call | solution.py:36
  167.8 7.0 %collective-permute-done.19.refs_2_ = bf16[128,512]{1,0:T(8,128)(2,1)S(1)} collective-permute-done((bf16[128,512]{1,0:T(8,128)(2,1)}, bf16[128,512]{1,0:T(8,128)(2,1)S(1)}, u32[]{:S(2)}, u32[]{:S(2)}) %collective-permute-start.19) | collective-permute-done | bytes 131104 | tf_op jit(solution)/shard_map/ppermute | solution.py:67
  175.5 2.3 %shard_map.76 = bf16[128,4096]{1,0:T(8,128)(2,1)} custom-call(s32[4]{0:T(128)} %pad_add_fusion.place, bf16[128,512]{1,0:T(8,128)(2,1)} %get-tuple-element.67.refs_0_, bf16[128,512]{1,0:T(8,128)(2,1)} %get-tuple-element.78.refs_1_, bf16[128,512]{1,0:T(8,128)(2,1)} %copy-done.20, bf16[128,512]{1,0:T(8,128)(2,1)} %copy-done.17, bf16[128,512]{1,0:T(8,128)(2,1)} %copy-done.21, ...), custom_call_target="tpu_custom_call" | custom-call | bytes 2097152 | tf_op jit(solution)/shard_map/pallas_call | solution.py:36
  (158 shorter events, 43.1 us)
Async XLA Ops:
  5.9 15.6 %collective-permute-start.15 = (bf16[128,1024]{1,0:T(8,128)(2,1)}, bf16[128,1024]{1,0:T(8,128)(2,1)S(1)}, u32[]{:S(2)}, u32[]{:S(2)}) collective-permute-start(bf16[128,1024]{1,0:T(8,128)(2,1)} %get-tuple-element.72), channel_id=1, source_target_pairs={{0,3},{1,2},{2,1},{3,0},{4,7},{5,6},{6,5},{7,4},{8,11},{9,10},{10,... | collective-permute-start | bytes 786440 | tf_op jit(solution)/shard_map/ppermute | solution.py:67
  8.4 35.3 %collective-permute-start.16 = (bf16[128,1024]{1,0:T(8,128)(2,1)}, bf16[128,1024]{1,0:T(8,128)(2,1)S(1)}, u32[]{:S(2)}, u32[]{:S(2)}) collective-permute-start(bf16[128,1024]{1,0:T(8,128)(2,1)} %get-tuple-element.73), channel_id=1, source_target_pairs={{0,2},{1,0},{2,3},{3,1},{4,6},{5,4},{6,7},{7,5},{8,10},{9,8},{10,1... | collective-permute-start | bytes 786440 | tf_op jit(solution)/shard_map/ppermute | solution.py:67
  12.2 39.0 %collective-permute-start = (bf16[128,1024]{1,0:T(8,128)(2,1)}, bf16[128,1024]{1,0:T(8,128)(2,1)S(1)}, u32[]{:S(2)}, u32[]{:S(2)}) collective-permute-start(bf16[128,1024]{1,0:T(8,128)(2,1)} %get-tuple-element.54), channel_id=1, source_target_pairs={{0,1},{1,3},{2,0},{3,2},{4,5},{5,7},{6,4},{7,6},{8,9},{9,11},{10,8... | collective-permute-start | bytes 786440 | tf_op jit(solution)/shard_map/ppermute | solution.py:67
  12.7 38.5 %collective-permute-start.1 = (bf16[128,1024]{1,0:T(8,128)(2,1)}, bf16[128,1024]{1,0:T(8,128)(2,1)S(1)}, u32[]{:S(2)}, u32[]{:S(2)}) collective-permute-start(bf16[128,1024]{1,0:T(8,128)(2,1)} %get-tuple-element.55), channel_id=1, source_target_pairs={{0,3},{1,2},{2,1},{3,0},{4,7},{5,6},{6,5},{7,4},{8,11},{9,10},{10,... | collective-permute-start | bytes 786440 | tf_op jit(solution)/shard_map/ppermute | solution.py:67
  15.8 46.5 %collective-permute-start.2 = (bf16[128,1024]{1,0:T(8,128)(2,1)}, bf16[128,1024]{1,0:T(8,128)(2,1)S(1)}, u32[]{:S(2)}, u32[]{:S(2)}) collective-permute-start(bf16[128,1024]{1,0:T(8,128)(2,1)} %get-tuple-element.56), channel_id=1, source_target_pairs={{0,2},{1,0},{2,3},{3,1},{4,6},{5,4},{6,7},{7,5},{8,10},{9,8},{10,1... | collective-permute-start | bytes 786440 | tf_op jit(solution)/shard_map/ppermute | solution.py:67
  21.5 49.4 %collective-permute-start.6 = (bf16[128,1024]{1,0:T(8,128)(2,1)S(1)}, bf16[128,1024]{1,0:T(8,128)(2,1)S(1)}, u32[]{:S(2)}, u32[]{:S(2)}) collective-permute-start(bf16[128,1024]{1,0:T(8,128)(2,1)S(1)} %copy-done.36), channel_id=1, source_target_pairs={{0,1},{1,3},{2,0},{3,2},{4,5},{5,7},{6,4},{7,6},{8,9},{9,11},{10,8... | collective-permute-start | bytes 786440 | tf_op jit(solution)/shard_map/ppermute | solution.py:67
  43.7 28.5 %collective-permute-start.7 = (bf16[128,1024]{1,0:T(8,128)(2,1)S(1)}, bf16[128,1024]{1,0:T(8,128)(2,1)S(1)}, u32[]{:S(2)}, u32[]{:S(2)}) collective-permute-start(bf16[128,1024]{1,0:T(8,128)(2,1)S(1)} %copy-done.34), channel_id=1, source_target_pairs={{0,3},{1,2},{2,1},{3,0},{4,7},{5,6},{6,5},{7,4},{8,11},{9,10},{10,... | collective-permute-start | bytes 786440 | tf_op jit(solution)/shard_map/ppermute | solution.py:67
  51.2 31.8 %collective-permute-start.17 = (bf16[512,512]{1,0:T(8,128)(2,1)}, bf16[512,512]{1,0:T(8,128)(2,1)S(1)}, u32[]{:S(2)}, u32[]{:S(2)}) collective-permute-start(bf16[512,512]{1,0:T(8,128)(2,1)} %get-tuple-element.75), channel_id=1, source_target_pairs={{0,4},{4,0},{8,12},{12,8},{16,20},{20,16},{24,28},{28,24},{1,5},{5... | collective-permute-start | bytes 1572872 | tf_op jit(solution)/shard_map/ppermute | solution.py:248
  51.2 21.1 %collective-permute-start.8 = (bf16[128,1024]{1,0:T(8,128)(2,1)S(1)}, bf16[128,1024]{1,0:T(8,128)(2,1)S(1)}, u32[]{:S(2)}, u32[]{:S(2)}) collective-permute-start(bf16[128,1024]{1,0:T(8,128)(2,1)S(1)} %copy-done.33), channel_id=1, source_target_pairs={{0,2},{1,0},{2,3},{3,1},{4,6},{5,4},{6,7},{7,5},{8,10},{9,8},{10,1... | collective-permute-start | bytes 786440 | tf_op jit(solution)/shard_map/ppermute | solution.py:67
  75.4 29.9 %collective-permute-start.9 = (bf16[512,512]{1,0:T(8,128)(2,1)}, bf16[512,512]{1,0:T(8,128)(2,1)S(1)}, u32[]{:S(2)}, u32[]{:S(2)}) collective-permute-start(bf16[512,512]{1,0:T(8,128)(2,1)} %get-tuple-element.64), channel_id=1, source_target_pairs={{0,4},{4,0},{8,12},{12,8},{16,20},{20,16},{24,28},{28,24},{1,5},{5... | collective-permute-start | bytes 1572872 | tf_op jit(solution)/shard_map/ppermute | solution.py:248
  75.9 24.8 %collective-permute-start.4 = (bf16[512,256]{1,0:T(8,128)(2,1)S(1)}, bf16[512,256]{1,0:T(8,128)(2,1)S(1)}, u32[]{:S(2)}, u32[]{:S(2)}) collective-permute-start(bf16[512,256]{1,0:T(8,128)(2,1)S(1)} %copy-done.35), channel_id=1, source_target_pairs={{0,12},{4,8},{8,20},{12,16},{16,28},{20,24},{1,13},{5,9},{9,21},{1... | collective-permute-start | bytes 786440 | tf_op jit(solution)/shard_map/ppermute | solution.py:248
  80.7 24.6 %collective-permute-start.5 = (bf16[512,256]{1,0:T(8,128)(2,1)S(1)}, bf16[512,256]{1,0:T(8,128)(2,1)S(1)}, u32[]{:S(2)}, u32[]{:S(2)}) collective-permute-start(bf16[512,256]{1,0:T(8,128)(2,1)S(1)} %copy-done.35), channel_id=1, source_target_pairs={{0,4},{4,0},{8,12},{12,8},{16,20},{20,16},{24,28},{28,24},{1,5},{5... | collective-permute-start | bytes 786440 | tf_op jit(solution)/shard_map/ppermute | solution.py:248
  81.5 19.1 %collective-permute-start.3 = (bf16[512,256]{1,0:T(8,128)(2,1)S(1)}, bf16[512,256]{1,0:T(8,128)(2,1)S(1)}, u32[]{:S(2)}, u32[]{:S(2)}) collective-permute-start(bf16[512,256]{1,0:T(8,128)(2,1)S(1)} %copy-done.32), channel_id=1, source_target_pairs={{0,8},{4,12},{8,16},{12,20},{16,24},{20,28},{1,9},{5,13},{9,17},{1... | collective-permute-start | bytes 786440 | tf_op jit(solution)/shard_map/ppermute | solution.py:248
  96.1 24.6 %collective-permute-start.28 = (bf16[512,256]{1,0:T(8,128)(2,1)}, bf16[512,256]{1,0:T(8,128)(2,1)S(1)}, u32[]{:S(2)}, u32[]{:S(2)}) collective-permute-start(bf16[512,256]{1,0:T(8,128)(2,1)} %get-tuple-element.91), channel_id=1, source_target_pairs={{8,0},{12,4},{16,8},{20,12},{24,16},{28,20},{9,1},{13,5},{17,9},{2... | collective-permute-start | bytes 786440 | tf_op jit(solution)/shard_map/ppermute | solution.py:248
  100.6 22.0 %collective-permute-start.29 = (bf16[512,256]{1,0:T(8,128)(2,1)}, bf16[512,256]{1,0:T(8,128)(2,1)S(1)}, u32[]{:S(2)}, u32[]{:S(2)}) collective-permute-start(bf16[512,256]{1,0:T(8,128)(2,1)} %get-tuple-element.92), channel_id=1, source_target_pairs={{0,4},{4,0},{8,12},{12,8},{16,20},{20,16},{24,28},{28,24},{1,5},{5... | collective-permute-start | bytes 786440 | tf_op jit(solution)/shard_map/ppermute | solution.py:248
  100.7 22.3 %collective-permute-start.30 = (bf16[512,256]{1,0:T(8,128)(2,1)}, bf16[512,256]{1,0:T(8,128)(2,1)S(1)}, u32[]{:S(2)}, u32[]{:S(2)}) collective-permute-start(bf16[512,256]{1,0:T(8,128)(2,1)} %get-tuple-element.93), channel_id=1, source_target_pairs={{8,4},{12,0},{16,12},{20,8},{24,20},{28,16},{9,5},{13,1},{17,13},{... | collective-permute-start | bytes 786440 | tf_op jit(solution)/shard_map/ppermute | solution.py:248
  122.7 15.8 %collective-permute-start.18 = (bf16[512,256]{1,0:T(8,128)(2,1)S(1)}, bf16[512,256]{1,0:T(8,128)(2,1)S(1)}, u32[]{:S(2)}, u32[]{:S(2)}) collective-permute-start(bf16[512,256]{1,0:T(8,128)(2,1)S(1)} %copy-done.31), channel_id=1, source_target_pairs={{0,4},{4,0},{8,12},{12,8},{16,20},{20,16},{24,28},{28,24},{1,5},{5... | collective-permute-start | bytes 786440 | tf_op jit(solution)/shard_map/ppermute | solution.py:248
  123.0 18.0 %collective-permute-start.10 = (bf16[512,256]{1,0:T(8,128)(2,1)}, bf16[512,256]{1,0:T(8,128)(2,1)S(1)}, u32[]{:S(2)}, u32[]{:S(2)}) collective-permute-start(bf16[512,256]{1,0:T(8,128)(2,1)} %get-tuple-element.66), channel_id=1, source_target_pairs={{0,4},{4,0},{8,12},{12,8},{16,20},{20,16},{24,28},{28,24},{1,5},{5... | collective-permute-start | bytes 786440 | tf_op jit(solution)/shard_map/ppermute | solution.py:248
  127.5 15.1 %collective-permute-start.32 = (bf16[128,512]{1,0:T(8,128)(2,1)}, bf16[128,512]{1,0:T(8,128)(2,1)S(1)}, u32[]{:S(2)}, u32[]{:S(2)}) collective-permute-start(bf16[128,512]{1,0:T(8,128)(2,1)} %get-tuple-element.96), channel_id=1, source_target_pairs={{0,1},{1,3},{2,0},{3,2},{4,5},{5,7},{6,4},{7,6},{8,9},{9,11},{10,8... | collective-permute-start | bytes 393224 | tf_op jit(solution)/shard_map/ppermute | solution.py:67
  138.5 16.0 %collective-permute-start.31 = (bf16[128,512]{1,0:T(8,128)(2,1)}, bf16[128,512]{1,0:T(8,128)(2,1)S(1)}, u32[]{:S(2)}, u32[]{:S(2)}) collective-permute-start(bf16[128,512]{1,0:T(8,128)(2,1)} %get-tuple-element.95), channel_id=1, source_target_pairs={{0,1},{1,3},{2,0},{3,2},{4,5},{5,7},{6,4},{7,6},{8,9},{9,11},{10,8... | collective-permute-start | bytes 393224 | tf_op jit(solution)/shard_map/ppermute | solution.py:67
  142.7 19.1 %collective-permute-start.35 = (bf16[128,512]{1,0:T(8,128)(2,1)S(1)}, bf16[128,512]{1,0:T(8,128)(2,1)S(1)}, u32[]{:S(2)}, u32[]{:S(2)}) collective-permute-start(bf16[128,512]{1,0:T(8,128)(2,1)S(1)} %copy-done.45), channel_id=1, source_target_pairs={{0,2},{1,0},{2,3},{3,1},{4,6},{5,4},{6,7},{7,5},{8,10},{9,8},{10,1... | collective-permute-start | bytes 393224 | tf_op jit(solution)/shard_map/ppermute | solution.py:67
  143.5 21.8 %collective-permute-start.20 = (bf16[128,512]{1,0:T(8,128)(2,1)}, bf16[128,512]{1,0:T(8,128)(2,1)S(1)}, u32[]{:S(2)}, u32[]{:S(2)}) collective-permute-start(bf16[128,512]{1,0:T(8,128)(2,1)} %get-tuple-element.80), channel_id=1, source_target_pairs={{0,1},{1,3},{2,0},{3,2},{4,5},{5,7},{6,4},{7,6},{8,9},{9,11},{10,8... | collective-permute-start | bytes 393224 | tf_op jit(solution)/shard_map/ppermute | solution.py:67
  146.7 21.1 %collective-permute-start.22 = (bf16[128,512]{1,0:T(8,128)(2,1)S(1)}, bf16[128,512]{1,0:T(8,128)(2,1)S(1)}, u32[]{:S(2)}, u32[]{:S(2)}) collective-permute-start(bf16[128,512]{1,0:T(8,128)(2,1)S(1)} %copy-done.44), channel_id=1, source_target_pairs={{0,3},{1,2},{2,1},{3,0},{4,7},{5,6},{6,5},{7,4},{8,11},{9,10},{10,... | collective-permute-start | bytes 393224 | tf_op jit(solution)/shard_map/ppermute | solution.py:67
  154.5 20.3 %collective-permute-start.19 = (bf16[128,512]{1,0:T(8,128)(2,1)}, bf16[128,512]{1,0:T(8,128)(2,1)S(1)}, u32[]{:S(2)}, u32[]{:S(2)}) collective-permute-start(bf16[128,512]{1,0:T(8,128)(2,1)} %get-tuple-element.79), channel_id=1, source_target_pairs={{0,1},{1,3},{2,0},{3,2},{4,5},{5,7},{6,4},{7,6},{8,9},{9,11},{10,8... | collective-permute-start | bytes 393224 | tf_op jit(solution)/shard_map/ppermute | solution.py:67
  (60 other events, 449.2 us)

commit v2 on v1

--- a/solution.py
+++ b/solution.py
@@ -99,7 +99,7 @@
     dq_outs = refs[kv_count + q_count : kv_count + 2 * q_count]
     kv_outs = refs[kv_count + 2 * q_count : 2 * kv_count + 2 * q_count]
     scratch = refs[2 * kv_count + 2 * q_count :]
-    q_rows, g_rows, keys, values, keys_t, score, d_att, att_low, d_low, dk, dv, dq_all = scratch
+    q_rows, g_rows, keys, values, keys_t, score, att_low, d_low, dk, dv, dq_all = scratch
     block = q_refs[0].shape[0]
     span = score.shape[0]
     tiles = span // TILE
@@ -118,7 +118,6 @@
     key_id = lax.broadcasted_iota(jnp.int32, (TILE, lanes), 0)
     row_id = jnp.bitwise_and(lax.broadcasted_iota(jnp.int32, (TILE, lanes), 1), TILE - 1)
     lower = key_id <= row_id
-    across_cols = (((1,), (1,)), ((), ()))
     exponent = jnp.float32(score_scale * LOG2_E)
 
     def fold(x):
@@ -134,36 +133,48 @@
             [g_rows[these, g * HEAD_DIM : (g + 1) * HEAD_DIM] for g in range(GROUPS)], axis=0
         )
         there = slice(base, base + span)
-        score[...] = lax.dot_general(
-            keys[there, :], q_two, across_cols, preferred_element_type=jnp.float32
-        )
-        d_att[...] = lax.dot_general(
-            values[there, :], g_two, across_cols, preferred_element_type=jnp.float32
-        )
-        score[0:TILE, :] = jnp.where(lower, -1e30, score[0:TILE, :])
-        score[span - TILE : span, :] = jnp.where(lower, score[span - TILE : span, :], -1e30)
+        q_t, g_t = q_two.T, g_two.T
+
+        def scores(t):
+            s = jnp.dot(
+                keys[base + t * TILE : base + (t + 1) * TILE, :],
+                q_t,
+                preferred_element_type=jnp.float32,
+            )
+            if t == 0:
+                s = jnp.where(lower, -1e30, s)
+            if t == tiles - 1:
+                s = jnp.where(lower, s, -1e30)
+            return s
+
+        def d_attention(t):
+            return jnp.dot(
+                values[base + t * TILE : base + (t + 1) * TILE, :],
+                g_t,
+                preferred_element_type=jnp.float32,
+            )
+
         top = jnp.full((8, lanes), -1e30, jnp.float32)
         for t in range(tiles):
-            s = score[t * TILE : (t + 1) * TILE, :]
             gone = jnp.where(base + t * TILE < first_key, -1e30, 0.0)
-            top = jnp.maximum(top, jnp.max(fold(s), axis=0) + gone)
+            top = jnp.maximum(top, jnp.max(fold(scores(t)), axis=0) + gone)
         top = jnp.max(top, axis=0, keepdims=True)
         total = jnp.zeros((8, lanes), jnp.float32)
         inner = jnp.zeros((8, lanes), jnp.float32)
         for t in range(tiles):
             here = slice(t * TILE, (t + 1) * TILE)
             level = top + jnp.where(base + t * TILE < first_key, 1e30, 0.0)
-            p = jnp.exp2((score[here, :] - level) * exponent)
+            p = jnp.exp2((scores(t) - level) * exponent)
             score[here, :] = p
             total = total + jnp.sum(fold(p), axis=0)
-            inner = inner + jnp.sum(fold(p * d_att[here, :]), axis=0)
+            inner = inner + jnp.sum(fold(p * d_attention(t)), axis=0)
         inverse = 1.0 / jnp.sum(total, axis=0, keepdims=True)
         center = jnp.sum(inner, axis=0, keepdims=True) * inverse
         for t in range(tiles):
             here = slice(t * TILE, (t + 1) * TILE)
             att = score[here, :] * inverse
             att_low[here, :] = att.astype(jnp.bfloat16)
-            d_low[here, :] = (att * (d_att[here, :] - center)).astype(jnp.bfloat16)
+            d_low[here, :] = (att * (d_attention(t) - center)).astype(jnp.bfloat16)
         dv[there, :] += jnp.dot(att_low[...], g_two, preferred_element_type=jnp.float32)
         dk[there, :] += jnp.dot(d_low[...], q_two, preferred_element_type=jnp.float32)
         dq_t = jnp.dot(keys_t[:, there], d_low[...], preferred_element_type=jnp.float32)
@@ -268,7 +279,6 @@
             pltpu.VMEM((key_count, HEAD_DIM), low),
             pltpu.VMEM((HEAD_DIM, key_count), low),
             pltpu.VMEM((span, lanes), wide),
-            pltpu.VMEM((span, lanes), wide),
             pltpu.VMEM((span, lanes), low),
             pltpu.VMEM((span, lanes), low),
             pltpu.VMEM((key_count, HEAD_DIM), wide),

time: 181 us -> 179 us (0.989)
  transfers between devices with their start and end apart: 37 -> 37, of which waited for: 8 -> 8; matrix products, arithmetic and copies ran while one was open for 0% -> 0% of each run, Pallas kernels for 25% -> 24%
where the time goes in v2:
time: 179 us; the launch traced here: 176 us
  starting transfers between devices  93.7 us (52%)
  Pallas kernels  48.4 us (27%)
  waiting for transfers between devices  26.5 us (15%)
  local copies, waits for them, and re-layouts  5.72 us (3%)
    ppermute x21, starting transfers between devices, across(): return lax.ppermute(shard, 'head', moves)  74.3 us
    pallas_call x13, Pallas kernels, local_call(): pl.pallas_call(body, out_shape=outs, in_specs=[smem()] + [vmem()] * (len(...  48.4 us
    ppermute x21, waiting for transfers between devices, across(): return lax.ppermute(shard, 'head', moves)  21.3 us
    ppermute x16, starting transfers between devices, ctx_moved(): return lax.ppermute(shard, 'ctx', moves)  19.5 us
    unnamed x94, local copies, waits for them, and re-layouts  5.72 us
    ppermute x16, waiting for transfers between devices, ctx_moved(): return lax.ppermute(shard, 'ctx', moves)  5.19 us
  transfers between devices with their start and end apart: 37, of which 8 were waited for; matrix products, arithmetic and copies ran while one was open for 0% of the time, Pallas kernels for 24%

profile of v2, /device:TPU:6, one launch (start us, length us, event | category | flops | bytes accessed | tf_op | source)
XLA Modules:
  0.0 176.1 jit_solution(11883224035355071412)
XLA Ops:
  1.3 3.0 %shard_map.69 = (bf16[128,1024]{1,0:T(8,128)(2,1)}, bf16[128,1024]{1,0:T(8,128)(2,1)}, bf16[128,1024]{1,0:T(8,128)(2,1)}, bf16[128,1024]{1,0:T(8,128)(2,1)}, bf1...) custom-call(s32[4]{0:T(128)} %pad_add_fusion.place, ...), custom_call_target="tpu_custom_call" | custom-call | bytes 4194304 | tf_op jit(solution)/shard_map/pallas_call | solution.py:36
  5.9 2.5 %collective-permute-start.15 = (bf16[128,1024]{1,0:T(8,128)(2,1)}, bf16[128,1024]{1,0:T(8,128)(2,1)S(1)}, u32[]{:S(2)}, u32[]{:S(2)}) collective-permute-start(bf16[128,1024]{1,0:T(8,128)(2,1)} %get-tuple-element.72), channel_id=1, source_target_pairs={{0,3},{1,2},{2,1},{3,0},{4,7},{5,6},{6,5},{7,4},{8,11},{9,10},{10,... | collective-permute-start | bytes 786440 | tf_op jit(solution)/shard_map/ppermute | solution.py:67
  10.0 2.3 %shard_map.67 = (bf16[128,1024]{1,0:T(8,128)(2,1)}, bf16[128,1024]{1,0:T(8,128)(2,1)}, bf16[128,1024]{1,0:T(8,128)(2,1)}, bf16[128,1024]{1,0:T(8,128)(2,1)}) custom-call(s32[4]{0:T(128)} %pad_add_fusion.place, bf16[128,2048]{1,0:T(8,128)(2,1)} %left.2, bf16[128,2048]{1,0:T(8,128)(2,1)} %right.2), custom_call_target="tpu_custom_call" | custom-call | bytes 2097152 | tf_op jit(solution)/shard_map/pallas_call | solution.py:36
  16.3 5.2 %collective-permute-done.15.refs_2_ = bf16[128,1024]{1,0:T(8,128)(2,1)S(1)} collective-permute-done((bf16[128,1024]{1,0:T(8,128)(2,1)}, bf16[128,1024]{1,0:T(8,128)(2,1)S(1)}, u32[]{:S(2)}, u32[]{:S(2)}) %collective-permute-start.15) | collective-permute-done | bytes 262176 | tf_op jit(solution)/shard_map/ppermute | solution.py:67
  21.5 22.2 %collective-permute-start.6 = (bf16[128,1024]{1,0:T(8,128)(2,1)S(1)}, bf16[128,1024]{1,0:T(8,128)(2,1)S(1)}, u32[]{:S(2)}, u32[]{:S(2)}) collective-permute-start(bf16[128,1024]{1,0:T(8,128)(2,1)S(1)} %copy-done.36), channel_id=1, source_target_pairs={{0,1},{1,3},{2,0},{3,2},{4,5},{5,7},{6,4},{7,6},{8,9},{9,11},{10,8... | collective-permute-start | bytes 786440 | tf_op jit(solution)/shard_map/ppermute | solution.py:67
  43.7 3.3 %collective-permute-start.7 = (bf16[128,1024]{1,0:T(8,128)(2,1)S(1)}, bf16[128,1024]{1,0:T(8,128)(2,1)S(1)}, u32[]{:S(2)}, u32[]{:S(2)}) collective-permute-start(bf16[128,1024]{1,0:T(8,128)(2,1)S(1)} %copy-done.34), channel_id=1, source_target_pairs={{0,3},{1,2},{2,1},{3,0},{4,7},{5,6},{6,5},{7,4},{8,11},{9,10},{10,... | collective-permute-start | bytes 786440 | tf_op jit(solution)/shard_map/ppermute | solution.py:67
  47.0 2.4 %shard_map.73 = (bf16[512,512]{1,0:T(8,128)(2,1)}, bf16[512,512]{1,0:T(8,128)(2,1)}) custom-call(s32[4]{0:T(128)} %pad_add_fusion.place, bf16[128,1024]{1,0:T(8,128)(2,1)} %get-tuple-element.70.refs_0_, bf16[128,1024]{1,0:T(8,128)(2,1)} %copy-done.13, bf16[128,1024]{1,0:T(8,128)(2,1)} %copy-done.14, bf16[128,1024]{1,0:T(8,128)(2,1)} %copy-done.16), custom_call_target="tpu_custom_call" | custom-call | bytes 2097152 | tf_op jit(solution)/shard_map/pallas_call | solution.py:36
  51.2 11.1 %collective-permute-start.8 = (bf16[128,1024]{1,0:T(8,128)(2,1)S(1)}, bf16[128,1024]{1,0:T(8,128)(2,1)S(1)}, u32[]{:S(2)}, u32[]{:S(2)}) collective-permute-start(bf16[128,1024]{1,0:T(8,128)(2,1)S(1)} %copy-done.33), channel_id=1, source_target_pairs={{0,2},{1,0},{2,3},{3,1},{4,6},{5,4},{6,7},{7,5},{8,10},{9,8},{10,1... | collective-permute-start | bytes 786440 | tf_op jit(solution)/shard_map/ppermute | solution.py:67
  63.0 2.4 %shard_map.68 = (bf16[512,256]{1,0:T(8,128)(2,1)}, bf16[512,256]{1,0:T(8,128)(2,1)}, bf16[512,256]{1,0:T(8,128)(2,1)}, bf16[512,256]{1,0:T(8,128)(2,1)}) custom-call(s32[4]{0:T(128)} %pad_add_fusion.place, bf16[128,1024]{1,0:T(8,128)(2,1)} %get-tuple-element.53.refs_0_, bf16[128,1024]{1,0:T(8,128)(2,1)} %copy-done.10, bf16[128,1024]{1,0:T(8,128)(2,1)} %copy-done.11, ...), custom_call_target="tpu_custom_call" | custom-call | bytes 2097152 | tf_op jit(solution)/shard_map/pallas_call | solution.py:36
  66.7 4.2 %collective-permute-done.6.refs_1_ = bf16[128,1024]{1,0:T(8,128)(2,1)S(1)} collective-permute-done((bf16[128,1024]{1,0:T(8,128)(2,1)S(1)}, bf16[128,1024]{1,0:T(8,128)(2,1)S(1)}, u32[]{:S(2)}, u32[]{:S(2)}) %collective-permute-start.6) | collective-permute-done | bytes 262176 | tf_op jit(solution)/shard_map/ppermute | solution.py:67
  73.0 2.4 %shard_map.70 = (bf16[512,512]{1,0:T(8,128)(2,1)}, bf16[512,512]{1,0:T(8,128)(2,1)}) custom-call(s32[4]{0:T(128)} %pad_add_fusion.place, bf16[128,1024]{1,0:T(8,128)(2,1)} %get-tuple-element.59.refs_0_, bf16[128,1024]{1,0:T(8,128)(2,1)} %copy-done.8, bf16[128,1024]{1,0:T(8,128)(2,1)} %copy-done.9, bf16[128,1024]{1,0:T(8,128)(2,1)} %copy-done.15), custom_call_target="tpu_custom_call" | custom-call | bytes 2097152 | tf_op jit(solution)/shard_map/pallas_call | solution.py:36
  77.2 3.5 %collective-permute-done.12.refs_1_ = bf16[512,256]{1,0:T(8,128)(2,1)S(1)} collective-permute-done((bf16[512,256]{1,0:T(8,128)(2,1)}, bf16[512,256]{1,0:T(8,128)(2,1)S(1)}, u32[]{:S(2)}, u32[]{:S(2)}) %collective-permute-start.12) | collective-permute-done | bytes 262176 | tf_op jit(solution)/shard_map/ppermute | solution.py:259
  83.6 11.6 %shard_map.74 = (bf16[512,256]{1,0:T(8,128)(2,1)}, bf16[512,256]{1,0:T(8,128)(2,1)}, bf16[512,256]{1,0:T(8,128)(2,1)}, bf16[512,256]{1,0:T(8,128)(2,1)}, f32[512,256]{1,0:T(8,128)}, /*index=5*/bf16[512,256]{1,0:T(8,128)(2,1)}) custom-call(s32[4]{0:T(128)} %pad_add_fusion.place, bf16[512,256]{1,0:T(8,128)(2,1)} %copy-done.38, bf16[512,256]{1,0:T(8,128)(2,1)} %copy-done.40, ...), custom_call_target="tpu_custom_call" | custom-call | flops 3019898880 | bytes 3932160 | tf_op jit(solution)/shard_map/pallas_call | solution.py:36
  95.1 4.5 %collective-permute-start.28 = (bf16[512,256]{1,0:T(8,128)(2,1)}, bf16[512,256]{1,0:T(8,128)(2,1)S(1)}, u32[]{:S(2)}, u32[]{:S(2)}) collective-permute-start(bf16[512,256]{1,0:T(8,128)(2,1)} %get-tuple-element.91), channel_id=1, source_target_pairs={{8,0},{12,4},{16,8},{20,12},{24,16},{28,20},{9,1},{13,5},{17,9},{2... | collective-permute-start | bytes 786440 | tf_op jit(solution)/shard_map/ppermute | solution.py:259
  99.8 4.5 %collective-permute-start.30 = (bf16[512,256]{1,0:T(8,128)(2,1)}, bf16[512,256]{1,0:T(8,128)(2,1)S(1)}, u32[]{:S(2)}, u32[]{:S(2)}) collective-permute-start(bf16[512,256]{1,0:T(8,128)(2,1)} %get-tuple-element.93), channel_id=1, source_target_pairs={{8,4},{12,0},{16,12},{20,8},{24,20},{28,16},{9,5},{13,1},{17,13},{... | collective-permute-start | bytes 786440 | tf_op jit(solution)/shard_map/ppermute | solution.py:259
  105.2 11.6 %shard_map.71 = (bf16[512,256]{1,0:T(8,128)(2,1)}, bf16[512,256]{1,0:T(8,128)(2,1)}, bf16[512,256]{1,0:T(8,128)(2,1)}, bf16[512,256]{1,0:T(8,128)(2,1)}, f32[512,256]{1,0:T(8,128)}, /*index=5*/bf16[512,256]{1,0:T(8,128)(2,1)}) custom-call(s32[4]{0:T(128)} %pad_add_fusion.place, bf16[512,256]{1,0:T(8,128)(2,1)} %copy-done.41, bf16[512,256]{1,0:T(8,128)(2,1)} %copy-done.37, ...), custom_call_target="tpu_custom_call" | custom-call | flops 3019898880 | bytes 3932160 | tf_op jit(solution)/shard_map/pallas_call | solution.py:36
  128.0 3.4 %collective-permute-start.34 = (bf16[128,512]{1,0:T(8,128)(2,1)}, bf16[128,512]{1,0:T(8,128)(2,1)S(1)}, u32[]{:S(2)}, u32[]{:S(2)}) collective-permute-start(bf16[128,512]{1,0:T(8,128)(2,1)} %get-tuple-element.98), channel_id=1, source_target_pairs={{0,3},{1,2},{2,1},{3,0},{4,7},{5,6},{6,5},{7,4},{8,11},{9,10},{10,... | collective-permute-start | bytes 393224 | tf_op jit(solution)/shard_map/ppermute | solution.py:67
  131.3 3.2 %collective-permute-start.36 = (bf16[128,512]{1,0:T(8,128)(2,1)}, bf16[128,512]{1,0:T(8,128)(2,1)S(1)}, u32[]{:S(2)}, u32[]{:S(2)}) collective-permute-start(bf16[128,512]{1,0:T(8,128)(2,1)} %get-tuple-element.100), channel_id=1, source_target_pairs={{0,2},{1,0},{2,3},{3,1},{4,6},{5,4},{6,7},{7,5},{8,10},{9,8},{10,1... | collective-permute-start | bytes 393224 | tf_op jit(solution)/shard_map/ppermute | solution.py:67
  144.9 6.4 %collective-permute-start.22 = (bf16[128,512]{1,0:T(8,128)(2,1)S(1)}, bf16[128,512]{1,0:T(8,128)(2,1)S(1)}, u32[]{:S(2)}, u32[]{:S(2)}) collective-permute-start(bf16[128,512]{1,0:T(8,128)(2,1)S(1)} %copy-done.44), channel_id=1, source_target_pairs={{0,3},{1,2},{2,1},{3,0},{4,7},{5,6},{6,5},{7,4},{8,11},{9,10},{10,... | collective-permute-start | bytes 393224 | tf_op jit(solution)/shard_map/ppermute | solution.py:67
  152.8 7.3 %collective-permute-start.19 = (bf16[128,512]{1,0:T(8,128)(2,1)}, bf16[128,512]{1,0:T(8,128)(2,1)S(1)}, u32[]{:S(2)}, u32[]{:S(2)}) collective-permute-start(bf16[128,512]{1,0:T(8,128)(2,1)} %get-tuple-element.79), channel_id=1, source_target_pairs={{0,1},{1,3},{2,0},{3,2},{4,5},{5,7},{6,4},{7,6},{8,9},{9,11},{10,8... | collective-permute-start | bytes 393224 | tf_op jit(solution)/shard_map/ppermute | solution.py:67
  160.1 3.5 %collective-permute-start.21 = (bf16[128,512]{1,0:T(8,128)(2,1)}, bf16[128,512]{1,0:T(8,128)(2,1)S(1)}, u32[]{:S(2)}, u32[]{:S(2)}) collective-permute-start(bf16[128,512]{1,0:T(8,128)(2,1)} %get-tuple-element.81), channel_id=1, source_target_pairs={{0,3},{1,2},{2,1},{3,0},{4,7},{5,6},{6,5},{7,4},{8,11},{9,10},{10,... | collective-permute-start | bytes 393224 | tf_op jit(solution)/shard_map/ppermute | solution.py:67
  163.6 2.4 %shard_map.79 = (bf16[128,2048]{1,0:T(8,128)(2,1)}, bf16[128,2048]{1,0:T(8,128)(2,1)}) custom-call(s32[4]{0:T(128)} %pad_add_fusion.place, bf16[128,512]{1,0:T(8,128)(2,1)} %get-tuple-element.89.refs_0_, bf16[128,512]{1,0:T(8,128)(2,1)} %get-tuple-element.94.refs_1_, bf16[128,512]{1,0:T(8,128)(2,1)} %copy-done.26, bf16[128,512]{1,0:T(8,128)(2,1)} %copy-done.23, ...), custom_call_target="tpu_custom_call" | custom-call | bytes 2097152 | tf_op jit(solution)/shard_map/pallas_call | solution.py:36
  166.1 7.0 %collective-permute-done.19.refs_2_ = bf16[128,512]{1,0:T(8,128)(2,1)S(1)} collective-permute-done((bf16[128,512]{1,0:T(8,128)(2,1)}, bf16[128,512]{1,0:T(8,128)(2,1)S(1)}, u32[]{:S(2)}, u32[]{:S(2)}) %collective-permute-start.19) | collective-permute-done | bytes 131104 | tf_op jit(solution)/shard_map/ppermute | solution.py:67
  173.8 2.3 %shard_map.76 = bf16[128,4096]{1,0:T(8,128)(2,1)} custom-call(s32[4]{0:T(128)} %pad_add_fusion.place, bf16[128,512]{1,0:T(8,128)(2,1)} %get-tuple-element.67.refs_0_, bf16[128,512]{1,0:T(8,128)(2,1)} %get-tuple-element.78.refs_1_, bf16[128,512]{1,0:T(8,128)(2,1)} %copy-done.20, bf16[128,512]{1,0:T(8,128)(2,1)} %copy-done.17, bf16[128,512]{1,0:T(8,128)(2,1)} %copy-done.21, ...), custom_call_target="tpu_custom_call" | custom-call | bytes 2097152 | tf_op jit(solution)/shard_map/pallas_call | solution.py:36
  (158 shorter events, 42.9 us)
Async XLA Ops:
  5.9 15.6 %collective-permute-start.15 = (bf16[128,1024]{1,0:T(8,128)(2,1)}, bf16[128,1024]{1,0:T(8,128)(2,1)S(1)}, u32[]{:S(2)}, u32[]{:S(2)}) collective-permute-start(bf16[128,1024]{1,0:T(8,128)(2,1)} %get-tuple-element.72), channel_id=1, source_target_pairs={{0,3},{1,2},{2,1},{3,0},{4,7},{5,6},{6,5},{7,4},{8,11},{9,10},{10,... | collective-permute-start | bytes 786440 | tf_op jit(solution)/shard_map/ppermute | solution.py:67
  8.4 35.3 %collective-permute-start.16 = (bf16[128,1024]{1,0:T(8,128)(2,1)}, bf16[128,1024]{1,0:T(8,128)(2,1)S(1)}, u32[]{:S(2)}, u32[]{:S(2)}) collective-permute-start(bf16[128,1024]{1,0:T(8,128)(2,1)} %get-tuple-element.73), channel_id=1, source_target_pairs={{0,2},{1,0},{2,3},{3,1},{4,6},{5,4},{6,7},{7,5},{8,10},{9,8},{10,1... | collective-permute-start | bytes 786440 | tf_op jit(solution)/shard_map/ppermute | solution.py:67
  12.2 39.0 %collective-permute-start = (bf16[128,1024]{1,0:T(8,128)(2,1)}, bf16[128,1024]{1,0:T(8,128)(2,1)S(1)}, u32[]{:S(2)}, u32[]{:S(2)}) collective-permute-start(bf16[128,1024]{1,0:T(8,128)(2,1)} %get-tuple-element.54), channel_id=1, source_target_pairs={{0,1},{1,3},{2,0},{3,2},{4,5},{5,7},{6,4},{7,6},{8,9},{9,11},{10,8... | collective-permute-start | bytes 786440 | tf_op jit(solution)/shard_map/ppermute | solution.py:67
  12.7 38.5 %collective-permute-start.1 = (bf16[128,1024]{1,0:T(8,128)(2,1)}, bf16[128,1024]{1,0:T(8,128)(2,1)S(1)}, u32[]{:S(2)}, u32[]{:S(2)}) collective-permute-start(bf16[128,1024]{1,0:T(8,128)(2,1)} %get-tuple-element.55), channel_id=1, source_target_pairs={{0,3},{1,2},{2,1},{3,0},{4,7},{5,6},{6,5},{7,4},{8,11},{9,10},{10,... | collective-permute-start | bytes 786440 | tf_op jit(solution)/shard_map/ppermute | solution.py:67
  15.8 46.5 %collective-permute-start.2 = (bf16[128,1024]{1,0:T(8,128)(2,1)}, bf16[128,1024]{1,0:T(8,128)(2,1)S(1)}, u32[]{:S(2)}, u32[]{:S(2)}) collective-permute-start(bf16[128,1024]{1,0:T(8,128)(2,1)} %get-tuple-element.56), channel_id=1, source_target_pairs={{0,2},{1,0},{2,3},{3,1},{4,6},{5,4},{6,7},{7,5},{8,10},{9,8},{10,1... | collective-permute-start | bytes 786440 | tf_op jit(solution)/shard_map/ppermute | solution.py:67
  21.5 49.4 %collective-permute-start.6 = (bf16[128,1024]{1,0:T(8,128)(2,1)S(1)}, bf16[128,1024]{1,0:T(8,128)(2,1)S(1)}, u32[]{:S(2)}, u32[]{:S(2)}) collective-permute-start(bf16[128,1024]{1,0:T(8,128)(2,1)S(1)} %copy-done.36), channel_id=1, source_target_pairs={{0,1},{1,3},{2,0},{3,2},{4,5},{5,7},{6,4},{7,6},{8,9},{9,11},{10,8... | collective-permute-start | bytes 786440 | tf_op jit(solution)/shard_map/ppermute | solution.py:67
  43.7 28.5 %collective-permute-start.7 = (bf16[128,1024]{1,0:T(8,128)(2,1)S(1)}, bf16[128,1024]{1,0:T(8,128)(2,1)S(1)}, u32[]{:S(2)}, u32[]{:S(2)}) collective-permute-start(bf16[128,1024]{1,0:T(8,128)(2,1)S(1)} %copy-done.34), channel_id=1, source_target_pairs={{0,3},{1,2},{2,1},{3,0},{4,7},{5,6},{6,5},{7,4},{8,11},{9,10},{10,... | collective-permute-start | bytes 786440 | tf_op jit(solution)/shard_map/ppermute | solution.py:67
  51.2 31.6 %collective-permute-start.17 = (bf16[512,512]{1,0:T(8,128)(2,1)}, bf16[512,512]{1,0:T(8,128)(2,1)S(1)}, u32[]{:S(2)}, u32[]{:S(2)}) collective-permute-start(bf16[512,512]{1,0:T(8,128)(2,1)} %get-tuple-element.75), channel_id=1, source_target_pairs={{0,4},{4,0},{8,12},{12,8},{16,20},{20,16},{24,28},{28,24},{1,5},{5... | collective-permute-start | bytes 1572872 | tf_op jit(solution)/shard_map/ppermute | solution.py:259
  51.2 21.1 %collective-permute-start.8 = (bf16[128,1024]{1,0:T(8,128)(2,1)S(1)}, bf16[128,1024]{1,0:T(8,128)(2,1)S(1)}, u32[]{:S(2)}, u32[]{:S(2)}) collective-permute-start(bf16[128,1024]{1,0:T(8,128)(2,1)S(1)} %copy-done.33), channel_id=1, source_target_pairs={{0,2},{1,0},{2,3},{3,1},{4,6},{5,4},{6,7},{7,5},{8,10},{9,8},{10,1... | collective-permute-start | bytes 786440 | tf_op jit(solution)/shard_map/ppermute | solution.py:67
  75.4 29.0 %collective-permute-start.9 = (bf16[512,512]{1,0:T(8,128)(2,1)}, bf16[512,512]{1,0:T(8,128)(2,1)S(1)}, u32[]{:S(2)}, u32[]{:S(2)}) collective-permute-start(bf16[512,512]{1,0:T(8,128)(2,1)} %get-tuple-element.64), channel_id=1, source_target_pairs={{0,4},{4,0},{8,12},{12,8},{16,20},{20,16},{24,28},{28,24},{1,5},{5... | collective-permute-start | bytes 1572872 | tf_op jit(solution)/shard_map/ppermute | solution.py:259
  75.9 23.9 %collective-permute-start.4 = (bf16[512,256]{1,0:T(8,128)(2,1)S(1)}, bf16[512,256]{1,0:T(8,128)(2,1)S(1)}, u32[]{:S(2)}, u32[]{:S(2)}) collective-permute-start(bf16[512,256]{1,0:T(8,128)(2,1)S(1)} %copy-done.35), channel_id=1, source_target_pairs={{0,12},{4,8},{8,20},{12,16},{16,28},{20,24},{1,13},{5,9},{9,21},{1... | collective-permute-start | bytes 786440 | tf_op jit(solution)/shard_map/ppermute | solution.py:259
  80.7 23.6 %collective-permute-start.5 = (bf16[512,256]{1,0:T(8,128)(2,1)S(1)}, bf16[512,256]{1,0:T(8,128)(2,1)S(1)}, u32[]{:S(2)}, u32[]{:S(2)}) collective-permute-start(bf16[512,256]{1,0:T(8,128)(2,1)S(1)} %copy-done.35), channel_id=1, source_target_pairs={{0,4},{4,0},{8,12},{12,8},{16,20},{20,16},{24,28},{28,24},{1,5},{5... | collective-permute-start | bytes 786440 | tf_op jit(solution)/shard_map/ppermute | solution.py:259
  81.5 18.2 %collective-permute-start.3 = (bf16[512,256]{1,0:T(8,128)(2,1)S(1)}, bf16[512,256]{1,0:T(8,128)(2,1)S(1)}, u32[]{:S(2)}, u32[]{:S(2)}) collective-permute-start(bf16[512,256]{1,0:T(8,128)(2,1)S(1)} %copy-done.32), channel_id=1, source_target_pairs={{0,8},{4,12},{8,16},{12,20},{16,24},{20,28},{1,9},{5,13},{9,17},{1... | collective-permute-start | bytes 786440 | tf_op jit(solution)/shard_map/ppermute | solution.py:259
  95.1 23.8 %collective-permute-start.28 = (bf16[512,256]{1,0:T(8,128)(2,1)}, bf16[512,256]{1,0:T(8,128)(2,1)S(1)}, u32[]{:S(2)}, u32[]{:S(2)}) collective-permute-start(bf16[512,256]{1,0:T(8,128)(2,1)} %get-tuple-element.91), channel_id=1, source_target_pairs={{8,0},{12,4},{16,8},{20,12},{24,16},{28,20},{9,1},{13,5},{17,9},{2... | collective-permute-start | bytes 786440 | tf_op jit(solution)/shard_map/ppermute | solution.py:259
  99.7 21.2 %collective-permute-start.29 = (bf16[512,256]{1,0:T(8,128)(2,1)}, bf16[512,256]{1,0:T(8,128)(2,1)S(1)}, u32[]{:S(2)}, u32[]{:S(2)}) collective-permute-start(bf16[512,256]{1,0:T(8,128)(2,1)} %get-tuple-element.92), channel_id=1, source_target_pairs={{0,4},{4,0},{8,12},{12,8},{16,20},{20,16},{24,28},{28,24},{1,5},{5... | collective-permute-start | bytes 786440 | tf_op jit(solution)/shard_map/ppermute | solution.py:259
  99.8 21.5 %collective-permute-start.30 = (bf16[512,256]{1,0:T(8,128)(2,1)}, bf16[512,256]{1,0:T(8,128)(2,1)S(1)}, u32[]{:S(2)}, u32[]{:S(2)}) collective-permute-start(bf16[512,256]{1,0:T(8,128)(2,1)} %get-tuple-element.93), channel_id=1, source_target_pairs={{8,4},{12,0},{16,12},{20,8},{24,20},{28,16},{9,5},{13,1},{17,13},{... | collective-permute-start | bytes 786440 | tf_op jit(solution)/shard_map/ppermute | solution.py:259
  120.9 15.8 %collective-permute-start.18 = (bf16[512,256]{1,0:T(8,128)(2,1)S(1)}, bf16[512,256]{1,0:T(8,128)(2,1)S(1)}, u32[]{:S(2)}, u32[]{:S(2)}) collective-permute-start(bf16[512,256]{1,0:T(8,128)(2,1)S(1)} %copy-done.31), channel_id=1, source_target_pairs={{0,4},{4,0},{8,12},{12,8},{16,20},{20,16},{24,28},{28,24},{1,5},{5... | collective-permute-start | bytes 786440 | tf_op jit(solution)/shard_map/ppermute | solution.py:259
  121.3 18.0 %collective-permute-start.10 = (bf16[512,256]{1,0:T(8,128)(2,1)}, bf16[512,256]{1,0:T(8,128)(2,1)S(1)}, u32[]{:S(2)}, u32[]{:S(2)}) collective-permute-start(bf16[512,256]{1,0:T(8,128)(2,1)} %get-tuple-element.66), channel_id=1, source_target_pairs={{0,4},{4,0},{8,12},{12,8},{16,20},{20,16},{24,28},{28,24},{1,5},{5... | collective-permute-start | bytes 786440 | tf_op jit(solution)/shard_map/ppermute | solution.py:259
  125.8 15.1 %collective-permute-start.32 = (bf16[128,512]{1,0:T(8,128)(2,1)}, bf16[128,512]{1,0:T(8,128)(2,1)S(1)}, u32[]{:S(2)}, u32[]{:S(2)}) collective-permute-start(bf16[128,512]{1,0:T(8,128)(2,1)} %get-tuple-element.96), channel_id=1, source_target_pairs={{0,1},{1,3},{2,0},{3,2},{4,5},{5,7},{6,4},{7,6},{8,9},{9,11},{10,8... | collective-permute-start | bytes 393224 | tf_op jit(solution)/shard_map/ppermute | solution.py:67
  136.7 16.0 %collective-permute-start.31 = (bf16[128,512]{1,0:T(8,128)(2,1)}, bf16[128,512]{1,0:T(8,128)(2,1)S(1)}, u32[]{:S(2)}, u32[]{:S(2)}) collective-permute-start(bf16[128,512]{1,0:T(8,128)(2,1)} %get-tuple-element.95), channel_id=1, source_target_pairs={{0,1},{1,3},{2,0},{3,2},{4,5},{5,7},{6,4},{7,6},{8,9},{9,11},{10,8... | collective-permute-start | bytes 393224 | tf_op jit(solution)/shard_map/ppermute | solution.py:67
  140.9 19.1 %collective-permute-start.35 = (bf16[128,512]{1,0:T(8,128)(2,1)S(1)}, bf16[128,512]{1,0:T(8,128)(2,1)S(1)}, u32[]{:S(2)}, u32[]{:S(2)}) collective-permute-start(bf16[128,512]{1,0:T(8,128)(2,1)S(1)} %copy-done.45), channel_id=1, source_target_pairs={{0,2},{1,0},{2,3},{3,1},{4,6},{5,4},{6,7},{7,5},{8,10},{9,8},{10,1... | collective-permute-start | bytes 393224 | tf_op jit(solution)/shard_map/ppermute | solution.py:67
  141.8 21.8 %collective-permute-start.20 = (bf16[128,512]{1,0:T(8,128)(2,1)}, bf16[128,512]{1,0:T(8,128)(2,1)S(1)}, u32[]{:S(2)}, u32[]{:S(2)}) collective-permute-start(bf16[128,512]{1,0:T(8,128)(2,1)} %get-tuple-element.80), channel_id=1, source_target_pairs={{0,1},{1,3},{2,0},{3,2},{4,5},{5,7},{6,4},{7,6},{8,9},{9,11},{10,8... | collective-permute-start | bytes 393224 | tf_op jit(solution)/shard_map/ppermute | solution.py:67
  144.9 21.1 %collective-permute-start.22 = (bf16[128,512]{1,0:T(8,128)(2,1)S(1)}, bf16[128,512]{1,0:T(8,128)(2,1)S(1)}, u32[]{:S(2)}, u32[]{:S(2)}) collective-permute-start(bf16[128,512]{1,0:T(8,128)(2,1)S(1)} %copy-done.44), channel_id=1, source_target_pairs={{0,3},{1,2},{2,1},{3,0},{4,7},{5,6},{6,5},{7,4},{8,11},{9,10},{10,... | collective-permute-start | bytes 393224 | tf_op jit(solution)/shard_map/ppermute | solution.py:67
  152.8 20.3 %collective-permute-start.19 = (bf16[128,512]{1,0:T(8,128)(2,1)}, bf16[128,512]{1,0:T(8,128)(2,1)S(1)}, u32[]{:S(2)}, u32[]{:S(2)}) collective-permute-start(bf16[128,512]{1,0:T(8,128)(2,1)} %get-tuple-element.79), channel_id=1, source_target_pairs={{0,1},{1,3},{2,0},{3,2},{4,5},{5,7},{6,4},{7,6},{8,9},{9,11},{10,8... | collective-permute-start | bytes 393224 | tf_op jit(solution)/shard_map/ppermute | solution.py:67
  (60 other events, 448.0 us)
